TPU v7x, 32 devices: a whole 2x2x4 slice. The times are simulated.
32 devices in a mesh: parts: 1, tile: 16 (over z, y, core), face: 2 (over x), sub: 1.
Axes of the slice: x: 2, y: 2, z: 4, core: 2. Of those that a mesh axis runs over, the one named last changes fastest.
Arguments:
- fields: bfloat16 [96, 4, 32, 96], P('sub', 'face', 'tile', 'parts'), may hold values from -6 to 6
- upstream: bfloat16 [96, 4, 32, 96], P('sub', 'face', 'tile', 'parts'), may hold values from -6 to 6
- kernel_one: bfloat16 [3, 3, 96, 96], replicated, may hold values from -0.21875 to 0.21875
- kernel_two: bfloat16 [3, 3, 96, 96], replicated, may hold values from -0.21875 to 0.21875
Outputs:
- result: bfloat16 [96, 4, 32, 96], P('sub', 'face', 'tile', 'parts')
- fields_grad: bfloat16 [96, 4, 32, 96], P('sub', 'face', 'tile', 'parts')
- kernel_one_grad: float32 [3, 3, 96, 96], P('parts', None, None, 'sub')
- kernel_two_grad: float32 [3, 3, 96, 96], P('parts', None, None, 'sub')
All inputs are finite; a program needn't handle non-finite values.
Results may differ from a plain program's by a relative error of at most 0.0049.
Values may be sent and summed in bfloat16 or wider, within the bound.
A program may use at most 128 MiB of HBM per device.

v0:
```python
import functools

import jax
import jax.numpy as jnp
from jax import lax
from jax.experimental import pallas as pl
from jax.experimental.pallas import tpu as pltpu
from jax.sharding import PartitionSpec as P

MESH = pl.DeviceIdType.MESH
F32 = jnp.float32
BF16 = jnp.bfloat16


def gelu_parts(v):
    root = 0.7978845608028654
    cube = 0.044715 * (v * v * v)
    th = jnp.tanh(root * (v + cube))
    value = v * (0.5 * (1.0 + th))
    slope = 0.5 * (1.0 + th) + 0.5 * v * (1.0 - th * th) * root * (1.0 + 0.134145 * (v * v))
    return value, slope


def product(a, b, da, db):
    return lax.dot_general(a, b, (((da,), (db,)), ((), ())), preferred_element_type=F32)


def body(n_t, n_f, scale, groups, fields_h, upstream_h, k1_h, k2_h, res_o, fg_o, w1_o, w2_o,
         x, k1, k2, y, rows, lh, rh, ap, bm, aps, tr, dr, tl, dl, al, pad, xb, xf1, xf2,
         acc, sbuf, rlow, rfull, obuf,
         col_s, col_r, a_s, a_r, b_s, b_r, t_s, t_r, d_s, d_r, w_s, w_r, in_s):
    _, G, J, H, C = x.shape
    S = H // 3
    E = J + 2
    t = lax.axis_index("tile")
    f = lax.axis_index("face")
    fn = lax.rem(f + 1, n_f)
    fp = lax.rem(f + n_f - 1, n_f)
    first = t == 0
    last = t == n_t - 1
    inner_left = jnp.logical_not(first)
    inner_right = jnp.logical_not(last)

    def where_to(tile, face):
        return {"tile": tile, "face": face}

    def remote(src, dst, s, r, dev):
        return pltpu.make_async_remote_copy(
            src_ref=src, dst_ref=dst, send_sem=s, recv_sem=r, device_id=dev, device_id_type=MESH)

    def copies(p, src):
        c0, cl = src.at[:, 0], src.at[:, J - 1]
        right = lambda: remote(cl, lh.at[p], col_s.at[p, 0], col_r.at[p, 0], where_to(jnp.minimum(t + 1, n_t - 1), f))
        left = lambda: remote(c0, rh.at[p], col_s.at[p, 1], col_r.at[p, 1], where_to(jnp.maximum(t - 1, 0), f))
        seam = []
        if G > 1:
            seam.append((first, lambda: remote(src.at[1:G, 0], rh.at[p, 0:G - 1], col_s.at[p, 2], col_r.at[p, 2], where_to(n_t - 1, f))))
            seam.append((last, lambda: remote(src.at[0:G - 1, J - 1], lh.at[p, 1:G], col_s.at[p, 3], col_r.at[p, 3], where_to(0, f))))
        seam.append((first, lambda: remote(src.at[0:1, 0], rh.at[p, G - 1:G], col_s.at[p, 4], col_r.at[p, 4], where_to(n_t - 1, fp))))
        seam.append((last, lambda: remote(src.at[G - 1:G, J - 1], lh.at[p, 0:1], col_s.at[p, 5], col_r.at[p, 5], where_to(0, fn))))
        a_own = lambda d: remote(aps.at[p, d, 1:G], ap.at[p, 0:G - 1], a_s.at[p, 0, d], a_r.at[p, 0], where_to(d, f))
        a_oth = lambda d: remote(aps.at[p, d, 0:1], ap.at[p, G - 1:G], a_s.at[p, 1, d], a_r.at[p, 1], where_to(d, fp))
        b_own = lambda d: remote(aps.at[p, d, 0:G - 1], bm.at[p, 1:G], b_s.at[p, 0, d], b_r.at[p, 0], where_to(d, f))
        b_oth = lambda d: remote(aps.at[p, d, G - 1:G], bm.at[p, 0:1], b_s.at[p, 1, d], b_r.at[p, 1], where_to(d, fn))
        t_own = lambda d: remote(rows.at[p, 0, 0:G - 1], tr.at[p, d, 1:G], t_s.at[p, 0], t_r.at[p, 0, d], where_to(0, f))
        t_oth = lambda d: remote(rows.at[p, 0, G - 1:G], tr.at[p, d, 0:1], t_s.at[p, 1], t_r.at[p, 1, d], where_to(0, fn))
        d_own = lambda d: remote(rows.at[p, 1, 1:G], dr.at[p, d, 0:G - 1], d_s.at[p, 0], d_r.at[p, 0, d], where_to(n_t - 1, f))
        d_oth = lambda d: remote(rows.at[p, 1, 0:1], dr.at[p, d, G - 1:G], d_s.at[p, 1], d_r.at[p, 1, d], where_to(n_t - 1, fp))
        return right, left, seam, a_own, a_oth, b_own, b_oth, t_own, t_oth, d_own, d_oth

    def stage(p, src):
        for q in range(G):
            for j in range(J):
                rows[p, 0, q, j:j + 1, :] = src[q, j, 0:16].astype(F32)[0:1]
                rows[p, 1, q, j:j + 1, :] = src[q, j, H - 16:H].astype(F32)[15:16]

        @pl.when(first)
        def _():
            more = 16 * (p % 2)
            for q in range(G):
                al[p % 2, q, 16:16 + S + more, :] = src[q, 0, 0:S + more].astype(F32)
            for d in range(n_t):
                aps[p, d] = al[p % 2, :, 15 + d * J:15 + d * J + E, :]

        @pl.when(last)
        def _():
            more = 16 * (p % 2)
            for q in range(G):
                al[p % 2, q, 16 - more:16 + S, :] = src[q, J - 1, 2 * S - more:H].astype(F32)
            for d in range(n_t):
                aps[p, d] = al[p % 2, :, 15 + d * J:15 + d * J + E, :]

    def start(p, src):
        right, left, seam, a_own, a_oth, b_own, b_oth, t_own, t_oth, d_own, d_oth = copies(p, src)
        t_oth(t).start()
        d_oth(t).start()
        if G > 1:
            @pl.when(inner_left)
            def _():
                t_own(t).start()

            @pl.when(inner_right)
            def _():
                d_own(t).start()
        for cond, make in seam:
            @pl.when(cond)
            def _(make=make):
                make().start()

        @pl.when(first)
        def _():
            @pl.loop(0, n_t)
            def _(d):
                a_oth(n_t - 1 - d).start()
            if G > 1:
                @pl.loop(1, n_t)
                def _(d):
                    a_own(n_t - d).start()
                ap[p, 0:G - 1] = aps[p, 0, 1:G]
                tr[p, 0, 1:G] = rows[p, 0, 0:G - 1]

        @pl.when(last)
        def _():
            @pl.loop(0, n_t)
            def _(d):
                b_oth(d).start()
            if G > 1:
                @pl.loop(0, n_t - 1)
                def _(d):
                    b_own(d).start()
                bm[p, 1:G] = aps[p, n_t - 1, 0:G - 1]
                dr[p, n_t - 1, 0:G - 1] = rows[p, 1, 1:G]

        @pl.when(inner_right)
        def _():
            right().start()

        @pl.when(inner_left)
        def _():
            left().start()

    def await_arrivals(p, src):
        right, left, seam, a_own, a_oth, b_own, b_oth, t_own, t_oth, d_own, d_oth = copies(p, src)

        @pl.when(inner_left)
        def _():
            right().wait_recv()
            if G > 1:
                a_own(0).wait_recv()

        @pl.when(inner_right)
        def _():
            left().wait_recv()
            if G > 1:
                b_own(0).wait_recv()

        for cond, make in seam:
            @pl.when(last if cond is first else first)
            def _(make=make):
                make().wait_recv()

        a_oth(0).wait_recv()
        b_oth(0).wait_recv()

        @pl.when(first)
        def _():
            if G > 1:
                @pl.loop(1, n_t)
                def _(d):
                    t_own(d).wait_recv()

            @pl.loop(0, n_t)
            def _(d):
                t_oth(d).wait_recv()
            for d in range(n_t):
                tl[p % 2, :, 8 + d * J:8 + (d + 1) * J, :] = tr[p, d]

        @pl.when(last)
        def _():
            if G > 1:
                @pl.loop(0, n_t - 1)
                def _(d):
                    d_own(d).wait_recv()

            @pl.loop(0, n_t)
            def _(d):
                d_oth(d).wait_recv()
            for d in range(n_t):
                dl[p % 2, :, 8 + d * J:8 + (d + 1) * J, :] = dr[p, d]

    def await_sends(p, src):
        right, left, seam, a_own, a_oth, b_own, b_oth, t_own, t_oth, d_own, d_oth = copies(p, src)

        @pl.when(inner_right)
        def _():
            right().wait_send()
            if G > 1:
                d_own(t).wait_send()

        @pl.when(inner_left)
        def _():
            left().wait_send()
            if G > 1:
                t_own(t).wait_send()

        for cond, make in seam:
            @pl.when(cond)
            def _(make=make):
                make().wait_send()
        t_oth(t).wait_send()
        d_oth(t).wait_send()

        @pl.when(first)
        def _():
            if G > 1:
                @pl.loop(1, n_t)
                def _(d):
                    a_own(d).wait_send()

            @pl.loop(0, n_t)
            def _(d):
                a_oth(d).wait_send()

        @pl.when(last)
        def _():
            if G > 1:
                @pl.loop(0, n_t - 1)
                def _(d):
                    b_own(d).wait_send()

            @pl.loop(0, n_t)
            def _(d):
                b_oth(d).wait_send()

    def fill_columns(src):
        for q in range(G):
            for j in range(J):
                pad[q, 1 + j, 8:8 + H, :] = src[q, j].astype(F32)

    def forward_taps(p, src, out):
        fill_columns(src)
        for q in range(G):
            @pl.when(inner_left)
            def _():
                pad[q, 0, 8:8 + H, :] = lh[p, q].astype(F32)

            @pl.when(first)
            def _():
                pad[q, 0, 8:8 + S, :] = tl[0, q, 8:8 + S, :]
                pad[q, 0, 8 + S:8 + H, :] = lh[p, q, 0:2 * S].astype(F32)

            @pl.when(inner_right)
            def _():
                pad[q, J + 1, 8:8 + H, :] = rh[p, q].astype(F32)

            @pl.when(last)
            def _():
                pad[q, J + 1, 8:8 + 2 * S, :] = rh[p, q, S:H].astype(F32)
                pad[q, J + 1, 8 + 2 * S:8 + H, :] = dl[0, q, 8:8 + S, :]
            for j in range(E):
                pad[q, j, 7:8, :] = ap[p, q, j:j + 1]
                pad[q, j, 8 + H:9 + H, :] = bm[p, q, j:j + 1]
        for a in range(3):
            for b in range(3):
                for q in range(G):
                    for j in range(J):
                        m = (q * J + j) * H
                        out[3 * a + b, m:m + H, :] = pad[q, j + a, 7 + b:7 + b + H, :].astype(BF16)

    def backward_taps(p, src, out):
        fill_columns(src)
        for q in range(G):
            @pl.when(inner_left)
            def _():
                pad[q, 0, 8:8 + H, :] = lh[p, q].astype(F32)

            @pl.when(first)
            def _():
                pad[q, 0, :, :] = jnp.zeros((H + 16, C), F32)

            @pl.when(inner_right)
            def _():
                pad[q, J + 1, 8:8 + H, :] = rh[p, q].astype(F32)

            @pl.when(last)
            def _():
                pad[q, J + 1, :, :] = jnp.zeros((H + 16, C), F32)
            for j in range(E):
                pad[q, j, 7:8, :] = jnp.zeros((1, C), F32)
                pad[q, j, 8 + H:9 + H, :] = jnp.zeros((1, C), F32)
        for a in range(3):
            for b in range(3):
                for q in range(G):
                    for j in range(J):
                        m = (q * J + j) * H
                        out[3 * a + b, m:m + H, :] = pad[q, j - a + 2, 9 - b:9 - b + H, :]
        for q in range(G):
            top = ap[p, q]
            low = bm[p, q]
            for b in range(3):
                for j in range(J):
                    m = (q * J + j) * H
                    out[b, m:m + 1, :] += top[j + 2 - b:j + 3 - b]
                    out[6 + b, m + H - 1:m + H, :] += low[j + 2 - b:j + 3 - b]

        @pl.when(last)
        def _():
            for q in range(G):
                m = (q * J + J - 1) * H
                pad[q, J + 1, 8:8 + H, :] = rh[p, q].astype(F32)
                for e in range(3):
                    out[e, m:m + 2 * S, :] += pad[q, J + 1, 8 + S + 1 - e:8 + H + 1 - e, :]
                    out[3 * e + 2, m + 2 * S:m + H, :] += dl[1, q, 9 - e:9 - e + S, :]

        @pl.when(first)
        def _():
            for q in range(G):
                m = q * J * H
                pad[q, 0, 8:8 + H, :] = lh[p, q].astype(F32)
                for e in range(3):
                    out[3 * e, m:m + S, :] += tl[1, q, 9 - e:9 - e + S, :]
                    out[6 + e, m + S:m + H, :] += pad[q, 0, 9 - e:9 - e + 2 * S, :]

    def apply(taps, k, dim):
        total = product(taps[0].astype(BF16), k[0, 0], 1, dim)
        for n in range(1, 9):
            total = total + product(taps[n].astype(BF16), k[n // 3, n % 3], 1, dim)
        return total

    def flat(src):
        return jnp.concatenate([src[q, j] for q in range(G) for j in range(J)], axis=0)

    def unflat(value, dst):
        for q in range(G):
            for j in range(J):
                m = (q * J + j) * H
                dst[q, j] = value[m:m + H]

    per = C // 16
    blocks = acc.shape[1]

    def weight_terms(taps, cot, w):
        for n in range(9):
            term = product(taps[n], cot, 0, 0) * scale
            acc[w, n * per:(n + 1) * per] = term.reshape(per, 16, C)

    class Sum:
        def __init__(self, w, out):
            self.out, self.at, self.over = out, 0, False
            self.w, self.lo, self.length, self.done = w, 0, blocks, []
            self.used = [0, 0]
            self.sem = 0

        def members(self, bits):
            mine, place = [], 0
            for axis, s in bits:
                mine.append(lax.rem((t if axis == "tile" else f) // s, 2))
            found = []
            for k in range(1, 2 ** len(bits)):
                tile, face, digit = t, f, 0
                for pos, (axis, s) in enumerate(bits):
                    bit = mine[pos]
                    if (k >> pos) & 1:
                        if axis == "tile":
                            tile = tile + (1 - 2 * bit) * s
                        else:
                            face = face + (1 - 2 * bit) * s
                        bit = 1 - bit
                    digit = digit + bit * (1 << pos)
                found.append((digit, where_to(tile, face)))
            own = 0
            for pos, bit in enumerate(mine):
                own = own + bit * (1 << pos)
            return own, found

        def begin(self, n):
            bits, full = groups[n]
            own, found = self.members(bits)
            part = self.length // (len(found) + 1)
            w = self.w
            inbox = rfull if full else rlow
            self.flying = []
            for digit, dev in found:
                give = self.lo + digit * part
                at = self.used[full]
                self.used[full] += part
                if full:
                    out = acc.at[w, pl.ds(give, part)]
                else:
                    sbuf[w, pl.ds(give, part)] = acc[w, pl.ds(give, part)].astype(BF16)
                    out = sbuf.at[w, pl.ds(give, part)]
                copy = remote(out, inbox.at[w, at:at + part], w_s.at[w, self.sem], w_r.at[w, self.sem], dev)
                self.sem += 1
                copy.start()
                self.flying.append((copy, inbox, at))
            keep = self.lo + own * part
            self.done.append((keep, part, found))
            self.lo, self.length = keep, part

        def end(self):
            total = acc[self.w, pl.ds(self.lo, self.length)]
            for copy, inbox, at in self.flying:
                copy.wait()
                total = total + inbox[self.w, at:at + self.length].astype(F32)
            acc[self.w, pl.ds(self.lo, self.length)] = total

        def round(self):
            obuf[self.w, pl.ds(self.lo, self.length)] = acc[self.w, pl.ds(self.lo, self.length)].astype(BF16)

        def give(self, n):
            keep, part, found = self.done[n]
            self.flying = []
            for digit, dev in found:
                copy = remote(obuf.at[self.w, pl.ds(keep, part)], obuf.at[self.w, pl.ds(keep, part)],
                              w_s.at[self.w, self.sem], w_r.at[self.w, self.sem], dev)
                self.sem += 1
                copy.start()
                self.flying.append(copy)

        def given(self):
            for copy in self.flying:
                copy.wait()

        def advance(self):
            at, count = self.at, len(groups)
            self.at += 1
            if at < count:
                if at > 0:
                    self.end()
                self.begin(at)
            elif at == count:
                self.end()
                self.round()
                self.give(count - 1)
            elif at < 2 * count:
                self.given()
                self.give(2 * count - 1 - at)
            elif at == 2 * count:
                self.given()
                for n in range(9):
                    self.out[n] = obuf[self.w, n * per:(n + 1) * per].reshape(C, C)
                self.over = True

    barrier = pltpu.get_barrier_semaphore()

    @pl.loop(0, n_f)
    def _(df):
        @pl.loop(0, n_t)
        def _(dt):
            @pl.when(jnp.logical_or(df != f, dt != t))
            def _():
                pl.semaphore_signal(barrier, inc=1, device_id=where_to(dt, df), device_id_type=MESH)
    loads = [pltpu.make_async_copy(src, dst, in_s.at[n]) for n, (src, dst) in enumerate(
        ((fields_h, x.at[0]), (upstream_h, x.at[1]), (k1_h, k1), (k2_h, k2)))]
    for load in loads:
        load.start()
    fields, upstream, hidden, pre_grad = x.at[0], x.at[1], y.at[0], y.at[1]
    al[...] = jnp.zeros_like(al)
    tl[...] = jnp.zeros_like(tl)
    dl[...] = jnp.zeros_like(dl)
    loads[0].wait()
    loads[1].wait()
    stage(0, fields)
    if blocks > 9 * per:
        for w in range(2):
            acc[w, 9 * per:blocks] = jnp.zeros((blocks - 9 * per, 16, C), F32)
    pl.semaphore_wait(barrier, n_t * n_f - 1)

    start(0, fields)
    stage(1, upstream)
    start(1, upstream)
    loads[2].wait()
    loads[3].wait()
    await_arrivals(0, fields)
    forward_taps(0, fields, xf1)
    value, slope = gelu_parts(apply(xf1, k1, 0))
    unflat(value.astype(BF16), hidden)
    stage(2, hidden)
    start(2, hidden)
    await_arrivals(1, upstream)
    backward_taps(1, upstream, xb)
    cot = (apply(xb, k2, 1) * slope).astype(BF16)
    unflat(cot, pre_grad)
    stage(3, pre_grad)
    start(3, pre_grad)
    one, two = Sum(0, w1_o), Sum(1, w2_o)
    cells = flat(hidden)
    for n in range(9):
        term = product(cells, xb[n].astype(BF16), 0, 0) * scale
        acc[1, n * per:(n + 1) * per] = term.reshape(per, 16, C)
    two.advance()
    weight_terms(xf1, cot, 0)
    one.advance()
    two.advance()
    one.advance()
    await_arrivals(2, hidden)
    forward_taps(2, hidden, xf2)
    unflat(apply(xf2, k2, 0).astype(BF16), res_o)
    two.advance()
    one.advance()
    await_arrivals(3, pre_grad)
    backward_taps(3, pre_grad, xb)
    unflat(apply(xb, k1, 1).astype(BF16), fg_o)
    while not (one.over and two.over):
        one.advance()
        two.advance()
    await_sends(0, fields)
    await_sends(1, upstream)
    await_sends(2, hidden)
    await_sends(3, pre_grad)


def plan(n_t, n_f):
    tile_bits = [1 << i for i in range(n_t.bit_length() - 1)]
    face_bits = [1 << i for i in range(n_f.bit_length() - 1)]
    groups = [([("tile", tile_bits[0])], 1)]
    middle = [("face", s) for s in face_bits] + [("tile", s) for s in tile_bits[1:2]]
    rest = [("tile", s) for s in tile_bits[2:]]
    while middle:
        groups.append((middle[:2], 0))
        middle = middle[2:]
    while rest:
        groups.append((rest[:2], 0))
        rest = rest[2:]
    return groups


def run(fields, upstream, k1, k2, n_t, n_f):
    G, J, H, C = fields.shape
    S = H // 3
    E = J + 2
    M = G * J * H
    ranks = n_t * n_f
    blocks = -(-(9 * (C // 16)) // ranks) * ranks
    scale = 1.0 / (S * 12.0 ** 0.5)
    groups = plan(n_t, n_f)
    length, room, flights = blocks, [1, 1], 0
    for bits, full in groups:
        others = 2 ** len(bits) - 1
        length //= others + 1
        room[full] += length * others
        flights += others
    dma = pltpu.SemaphoreType.DMA
    vmem = pl.BlockSpec(memory_space=pltpu.VMEM)
    return pl.pallas_call(
        functools.partial(body, n_t, n_f, scale, groups),
        out_shape=(
            jax.ShapeDtypeStruct((G, J, H, C), BF16),
            jax.ShapeDtypeStruct((G, J, H, C), BF16),
            jax.ShapeDtypeStruct((9, C, C), BF16),
            jax.ShapeDtypeStruct((9, C, C), BF16),
        ),
        in_specs=[pl.BlockSpec(memory_space=pl.ANY)] * 2 + [pl.BlockSpec(memory_space=pltpu.HBM)] * 2,
        out_specs=[vmem] * 4,
        scratch_shapes=[
            pltpu.VMEM((2, G, J, H, C), BF16),
            pltpu.VMEM(k1.shape, BF16),
            pltpu.VMEM(k2.shape, BF16),
            pltpu.VMEM((2, G, J, H, C), BF16),
            pltpu.VMEM((4, 2, G, J, C), F32),
            pltpu.VMEM((4, G, H, C), BF16),
            pltpu.VMEM((4, G, H, C), BF16),
            pltpu.VMEM((4, G, E, C), F32),
            pltpu.VMEM((4, G, E, C), F32),
            pltpu.VMEM((4, n_t, G, E, C), F32),
            pltpu.VMEM((4, n_t, G, J, C), F32),
            pltpu.VMEM((4, n_t, G, J, C), F32),
            pltpu.VMEM((2, G, S + 16, C), F32),
            pltpu.VMEM((2, G, S + 16, C), F32),
            pltpu.VMEM((2, G, S + 32, C), F32),
            pltpu.VMEM((G, J + 2, H + 16, C), F32),
            pltpu.VMEM((9, M, C), F32),
            pltpu.VMEM((9, M, C), BF16),
            pltpu.VMEM((9, M, C), BF16),
            pltpu.VMEM((2, blocks, 16, C), F32),
            pltpu.VMEM((2, blocks, 16, C), BF16),
            pltpu.VMEM((2, room[0], 16, C), BF16),
            pltpu.VMEM((2, room[1], 16, C), F32),
            pltpu.VMEM((2, blocks, 16, C), BF16),
            dma((4, 6)), dma((4, 6)),
            dma((4, 2, n_t)), dma((4, 2)),
            dma((4, 2, n_t)), dma((4, 2)),
            dma((4, 2)), dma((4, 2, n_t)),
            dma((4, 2)), dma((4, 2, n_t)),
            dma((2, 2 * flights)), dma((2, 2 * flights)), dma((4,)),
        ],
        compiler_params=pltpu.CompilerParams(
            collective_id=0, has_side_effects=True, vmem_limit_bytes=24 * 1024 * 1024),
    )(fields, upstream, pltpu.with_memory_space_constraint(k1, pltpu.HBM), pltpu.with_memory_space_constraint(k2, pltpu.HBM))


def on_device(n_sub, n_t, n_f, fields, upstream, k1, k2):
    own = fields.shape[0]
    if n_sub > 1:
        fields = lax.all_gather(fields, "sub", axis=0, tiled=True)
        upstream = lax.all_gather(upstream, "sub", axis=0, tiled=True)
    res, fgrad, w1, w2 = run(
        fields.transpose(1, 2, 3, 0), upstream.transpose(1, 2, 3, 0), k1, k2, n_t, n_f)
    if n_sub > 1:
        at = lax.axis_index("sub") * own
        res = lax.dynamic_slice_in_dim(res, at, own, 3)
        fgrad = lax.dynamic_slice_in_dim(fgrad, at, own, 3)
        w1 = lax.dynamic_slice_in_dim(w1, at, own, 2)
        w2 = lax.dynamic_slice_in_dim(w2, at, own, 2)
    shape = (3, 3) + w1.shape[1:]
    return (res.transpose(3, 0, 1, 2), fgrad.transpose(3, 0, 1, 2), w1.astype(F32).reshape(shape), w2.astype(F32).reshape(shape))


def solution(mesh):
    placed = (P("sub", "face", "tile", "parts"), P("sub", "face", "tile", "parts"), P(), P())
    sizes = mesh.shape
    return jax.shard_map(
        functools.partial(on_device, sizes["sub"], sizes["tile"], sizes["face"]),
        mesh=mesh,
        in_specs=placed,
        out_specs=(
            P("sub", "face", "tile", "parts"),
            P("sub", "face", "tile", "parts"),
            P("parts", None, None, "sub"),
            P("parts", None, None, "sub"),
        ),
        check_vma=False,
    )
```

profile of v0, /device:TPU:0, one launch (start us, length us, event | category | flops | bytes accessed | tf_op | source)
XLA Modules:
  0.0 44.3 jit_solution(2806837238087148219)
XLA Ops:
  0.6 0.0 copy-start
  0.6 1.0 %copy.8 = bf16[96,2,2,96]{0,3,2,1:T(8,128)(2,1)S(1)} copy(bf16[96,2,2,96]{3,2,1,0:T(2,128)(2,1)} %param.4) | data formatting | bytes 147456 | tf_op args[0]
  1.7 0.0 copy-done
  1.7 0.1 copy.9
  1.8 39.4 %shard_map.75 = (bf16[2,2,96,96]{3,2,1,0:T(8,128)(2,1)S(1)}, bf16[2,2,96,96]{3,2,1,0:T(8,128)(2,1)S(1)}, bf16[9,96,96]{2,1,0:T(8,128)(2,1)S(1)}, bf16[9,96,96]{2,1,0:T(8,128)(2,1)S(1)}) custom-call(bf16[2,2,96,96]{3,2,1,0:T(8,128)(2,1)S(1)} %bitcast.8, bf16[2,2,96,96]{3,2,1,0:T(8,128)(2,1)S(1)} %bitcast.9, bf16[3,3,96,96]{3,2,1,0:T(8,128)(2,1)} %k1_h.1, ...), custom_call_target="tpu_custom_call" | custom-call | tf_op jit(solution)/shard_map/pallas_call | solution.py:545
  41.2 0.8 %copy.10 = bf16[96,2,2,96]{3,2,1,0:T(2,128)(2,1)} copy(bf16[96,2,2,96]{0,3,2,1:T(8,128)(2,1)S(1)} %bitcast.13) | data formatting | bytes 147456
  42.0 0.8 %copy.11 = bf16[96,2,2,96]{3,2,1,0:T(2,128)(2,1)} copy(bf16[96,2,2,96]{0,3,2,1:T(8,128)(2,1)S(1)} %bitcast.12) | data formatting | bytes 147456
  42.7 0.8 %convert.2 = f32[3,3,96,96]{3,2,1,0:T(8,128)} convert(bf16[3,3,96,96]{3,2,1,0:T(8,128)(2,1)S(1)} %bitcast.11) | non-fusion elementwise | flops 82944 | bytes 497664 | tf_op jit(solution)/shard_map/reshape | solution.py:606
  43.5 0.8 %convert.3 = f32[3,3,96,96]{3,2,1,0:T(8,128)} convert(bf16[3,3,96,96]{3,2,1,0:T(8,128)(2,1)S(1)} %bitcast.10) | non-fusion elementwise | flops 82944 | bytes 497664 | tf_op jit(solution)/shard_map/reshape | solution.py:606
Async XLA Ops:
  0.6 1.1 %copy-start = (bf16[96,2,2,96]{3,2,1,0:T(2,128)(2,1)S(1)}, bf16[96,2,2,96]{3,2,1,0:T(2,128)(2,1)}, u32[]{:S(2)}) copy-start(bf16[96,2,2,96]{3,2,1,0:T(2,128)(2,1)} %param.5) | copy-start | bytes 221188
where the time goes:
time: 44.5 us; the launch traced here: 44.3 us
  Pallas kernels  39.4 us (89%)
  local copies, waits for them, and re-layouts  2.67 us (6%)
  other arithmetic  1.59 us (4%)
  between operations  0.66 us (1%)
    pallas_call x1, Pallas kernels, run(): pl.pallas_call(functools.partial(body, n_t, n_f, scale, groups), out_shap...  39.4 us
    unnamed x6, local copies, waits for them, and re-layouts  2.67 us

commit v1 on v0

v1 whole, which is shorter than its diff:
```python
import functools

import jax
import jax.numpy as jnp
from jax import lax
from jax.experimental import pallas as pl
from jax.experimental.pallas import tpu as pltpu
from jax.sharding import PartitionSpec as P

MESH = pl.DeviceIdType.MESH
F32 = jnp.float32
BF16 = jnp.bfloat16


def gelu_parts(v):
    root = 0.7978845608028654
    cube = 0.044715 * (v * v * v)
    th = jnp.tanh(root * (v + cube))
    value = v * (0.5 * (1.0 + th))
    slope = 0.5 * (1.0 + th) + 0.5 * v * (1.0 - th * th) * root * (1.0 + 0.134145 * (v * v))
    return value, slope


def product(a, b, da, db):
    return lax.dot_general(a, b, (((da,), (db,)), ((), ())), preferred_element_type=F32)


def body(n_t, n_f, scale, groups, fields_h, upstream_h, k1_h, k2_h, res_o, fg_o, w1_o, w2_o,
         raw, x, k1, k2, y, rows, lh, rh, ap, bm, aps, tr, dr, tl, dl, al, pad, xb, xf1, xf2,
         acc, sbuf, rlow, rfull, obuf,
         col_s, col_r, line_s, a_r, b_r, t_s, d_s, row_r, w_s, w_r, in_s):
    _, G, J, H, C = x.shape
    S = H // 3
    E = J + 2
    t = lax.axis_index("tile")
    f = lax.axis_index("face")
    fn = lax.rem(f + 1, n_f)
    fp = lax.rem(f + n_f - 1, n_f)
    first = t == 0
    last = t == n_t - 1
    inner_left = jnp.logical_not(first)
    inner_right = jnp.logical_not(last)

    def where_to(tile, face):
        return {"tile": tile, "face": face}

    def remote(src, dst, s, r, dev):
        return pltpu.make_async_remote_copy(
            src_ref=src, dst_ref=dst, send_sem=s, recv_sem=r, device_id=dev, device_id_type=MESH)

    def settle(ref, sem):
        pltpu.make_async_copy(ref, ref, sem).wait()

    def copies(p, src):
        c0, cl = src.at[:, :, 0], src.at[:, :, J - 1]
        right = lambda: remote(cl, lh.at[p], col_s.at[p, 0], col_r.at[p, 0], where_to(jnp.minimum(t + 1, n_t - 1), f))
        left = lambda: remote(c0, rh.at[p], col_s.at[p, 1], col_r.at[p, 1], where_to(jnp.maximum(t - 1, 0), f))
        seam = []
        if G > 1:
            seam.append((first, lambda: remote(src.at[:, 1:G, 0], rh.at[p, :, 0:G - 1], col_s.at[p, 2], col_r.at[p, 2], where_to(n_t - 1, f))))
            seam.append((last, lambda: remote(src.at[:, 0:G - 1, J - 1], lh.at[p, :, 1:G], col_s.at[p, 2], col_r.at[p, 2], where_to(0, f))))
        seam.append((first, lambda: remote(src.at[:, 0:1, 0], rh.at[p, :, G - 1:G], col_s.at[p, 3], col_r.at[p, 3], where_to(n_t - 1, fp))))
        seam.append((last, lambda: remote(src.at[:, G - 1:G, J - 1], lh.at[p, :, 0:1], col_s.at[p, 3], col_r.at[p, 3], where_to(0, fn))))
        a_own = lambda d: remote(aps.at[p, d, :, 1:G], ap.at[p, :, 0:G - 1], line_s.at[p, 0], a_r.at[p, 0], where_to(d, f))
        a_oth = lambda d: remote(aps.at[p, d, :, 0:1], ap.at[p, :, G - 1:G], line_s.at[p, 1], a_r.at[p, 1], where_to(d, fp))
        b_own = lambda d: remote(aps.at[p, d, :, 0:G - 1], bm.at[p, :, 1:G], line_s.at[p, 0], b_r.at[p, 0], where_to(d, f))
        b_oth = lambda d: remote(aps.at[p, d, :, G - 1:G], bm.at[p, :, 0:1], line_s.at[p, 1], b_r.at[p, 1], where_to(d, fn))
        t_own = lambda d: remote(rows.at[p, 0, :, 0:G - 1], tr.at[p, d, :, 1:G], t_s.at[p, 0], row_r.at[p, 0], where_to(0, f))
        t_oth = lambda d: remote(rows.at[p, 0, :, G - 1:G], tr.at[p, d, :, 0:1], t_s.at[p, 1], row_r.at[p, 1], where_to(0, fn))
        d_own = lambda d: remote(rows.at[p, 1, :, 1:G], dr.at[p, d, :, 0:G - 1], d_s.at[p, 0], row_r.at[p, 0], where_to(n_t - 1, f))
        d_oth = lambda d: remote(rows.at[p, 1, :, 0:1], dr.at[p, d, :, G - 1:G], d_s.at[p, 1], row_r.at[p, 1], where_to(n_t - 1, fp))
        return right, left, seam, a_own, a_oth, b_own, b_oth, t_own, t_oth, d_own, d_oth

    def stage(p, kind, src):
        for q in range(G):
            for j in range(J):
                rows[p, 0, kind, q, j:j + 1, :] = src[kind, q, j, 0:16].astype(F32)[0:1]
                rows[p, 1, kind, q, j:j + 1, :] = src[kind, q, j, H - 16:H].astype(F32)[15:16]
        more = 16 * kind

        @pl.when(first)
        def _():
            for q in range(G):
                al[kind, q, 16:16 + S + more, :] = src[kind, q, 0, 0:S + more].astype(F32)
            for d in range(n_t):
                aps[p, d, kind] = al[kind, :, 15 + d * J:15 + d * J + E, :]

        @pl.when(last)
        def _():
            for q in range(G):
                al[kind, q, 16 - more:16 + S, :] = src[kind, q, J - 1, 2 * S - more:H].astype(F32)
            for d in range(n_t):
                aps[p, d, kind] = al[kind, :, 15 + d * J:15 + d * J + E, :]

    def start(p, src):
        right, left, seam, a_own, a_oth, b_own, b_oth, t_own, t_oth, d_own, d_oth = copies(p, src)
        t_oth(t).start()
        d_oth(t).start()
        if G > 1:
            @pl.when(inner_left)
            def _():
                t_own(t).start()

            @pl.when(inner_right)
            def _():
                d_own(t).start()
        for cond, make in seam:
            @pl.when(cond)
            def _(make=make):
                make().start()

        @pl.when(first)
        def _():
            @pl.loop(0, n_t)
            def _(d):
                a_oth(n_t - 1 - d).start()
            if G > 1:
                @pl.loop(1, n_t)
                def _(d):
                    a_own(n_t - d).start()
                ap[p, :, 0:G - 1] = aps[p, 0, :, 1:G]
                tr[p, 0, :, 1:G] = rows[p, 0, :, 0:G - 1]

        @pl.when(last)
        def _():
            @pl.loop(0, n_t)
            def _(d):
                b_oth(d).start()
            if G > 1:
                @pl.loop(0, n_t - 1)
                def _(d):
                    b_own(d).start()
                bm[p, :, 1:G] = aps[p, n_t - 1, :, 0:G - 1]
                dr[p, n_t - 1, :, 0:G - 1] = rows[p, 1, :, 1:G]

        @pl.when(inner_right)
        def _():
            right().start()

        @pl.when(inner_left)
        def _():
            left().start()

    def await_arrivals(p, src):
        right, left, seam, a_own, a_oth, b_own, b_oth, t_own, t_oth, d_own, d_oth = copies(p, src)

        @pl.when(inner_left)
        def _():
            right().wait_recv()
            if G > 1:
                a_own(0).wait_recv()

        @pl.when(inner_right)
        def _():
            left().wait_recv()
            if G > 1:
                b_own(0).wait_recv()

        for cond, make in seam:
            @pl.when(last if cond is first else first)
            def _(make=make):
                make().wait_recv()

        a_oth(0).wait_recv()
        b_oth(0).wait_recv()

        @pl.when(first)
        def _():
            if G > 1:
                settle(tr.at[p, 1:n_t, :, 1:G], row_r.at[p, 0])
            settle(tr.at[p, :, :, 0:1], row_r.at[p, 1])
            for d in range(n_t):
                tl[:, :, 8 + d * J:8 + (d + 1) * J, :] = tr[p, d]

        @pl.when(last)
        def _():
            if G > 1:
                settle(dr.at[p, 0:n_t - 1, :, 0:G - 1], row_r.at[p, 0])
            settle(dr.at[p, :, :, G - 1:G], row_r.at[p, 1])
            for d in range(n_t):
                dl[:, :, 8 + d * J:8 + (d + 1) * J, :] = dr[p, d]

    def await_sends(p, src):
        right, left, seam, a_own, a_oth, b_own, b_oth, t_own, t_oth, d_own, d_oth = copies(p, src)

        @pl.when(inner_right)
        def _():
            right().wait_send()
            if G > 1:
                d_own(t).wait_send()

        @pl.when(inner_left)
        def _():
            left().wait_send()
            if G > 1:
                t_own(t).wait_send()

        for cond, make in seam:
            @pl.when(cond)
            def _(make=make):
                make().wait_send()
        t_oth(t).wait_send()
        d_oth(t).wait_send()

        @pl.when(jnp.logical_or(first, last))
        def _():
            if G > 1:
                settle(aps.at[p, 1:n_t, :, 1:G], line_s.at[p, 0])
            settle(aps.at[p, :, :, 0:1], line_s.at[p, 1])

    def fill_columns(src):
        for q in range(G):
            for j in range(J):
                pad[q, 1 + j, 8:8 + H, :] = src[q, j].astype(F32)

    def forward_taps(p, src, out):
        fill_columns(src)
        for q in range(G):
            @pl.when(inner_left)
            def _():
                pad[q, 0, 8:8 + H, :] = lh[p, 0, q].astype(F32)

            @pl.when(first)
            def _():
                pad[q, 0, 8:8 + S, :] = tl[0, q, 8:8 + S, :]
                pad[q, 0, 8 + S:8 + H, :] = lh[p, 0, q, 0:2 * S].astype(F32)

            @pl.when(inner_right)
            def _():
                pad[q, J + 1, 8:8 + H, :] = rh[p, 0, q].astype(F32)

            @pl.when(last)
            def _():
                pad[q, J + 1, 8:8 + 2 * S, :] = rh[p, 0, q, S:H].astype(F32)
                pad[q, J + 1, 8 + 2 * S:8 + H, :] = dl[0, q, 8:8 + S, :]
            for j in range(E):
                pad[q, j, 7:8, :] = ap[p, 0, q, j:j + 1]
                pad[q, j, 8 + H:9 + H, :] = bm[p, 0, q, j:j + 1]
        for a in range(3):
            for b in range(3):
                for q in range(G):
                    for j in range(J):
                        m = (q * J + j) * H
                        out[3 * a + b, m:m + H, :] = pad[q, j + a, 7 + b:7 + b + H, :].astype(BF16)

    def backward_taps(p, src, out):
        fill_columns(src)
        for q in range(G):
            @pl.when(inner_left)
            def _():
                pad[q, 0, 8:8 + H, :] = lh[p, 1, q].astype(F32)

            @pl.when(first)
            def _():
                pad[q, 0, :, :] = jnp.zeros((H + 16, C), F32)

            @pl.when(inner_right)
            def _():
                pad[q, J + 1, 8:8 + H, :] = rh[p, 1, q].astype(F32)

            @pl.when(last)
            def _():
                pad[q, J + 1, :, :] = jnp.zeros((H + 16, C), F32)
            for j in range(E):
                pad[q, j, 7:8, :] = jnp.zeros((1, C), F32)
                pad[q, j, 8 + H:9 + H, :] = jnp.zeros((1, C), F32)
        for a in range(3):
            for b in range(3):
                for q in range(G):
                    for j in range(J):
                        m = (q * J + j) * H
                        out[3 * a + b, m:m + H, :] = pad[q, j - a + 2, 9 - b:9 - b + H, :]
        for q in range(G):
            top = ap[p, 1, q]
            low = bm[p, 1, q]
            for b in range(3):
                for j in range(J):
                    m = (q * J + j) * H
                    out[b, m:m + 1, :] += top[j + 2 - b:j + 3 - b]
                    out[6 + b, m + H - 1:m + H, :] += low[j + 2 - b:j + 3 - b]

        @pl.when(last)
        def _():
            for q in range(G):
                m = (q * J + J - 1) * H
                pad[q, J + 1, 8:8 + H, :] = rh[p, 1, q].astype(F32)
                for e in range(3):
                    out[e, m:m + 2 * S, :] += pad[q, J + 1, 8 + S + 1 - e:8 + H + 1 - e, :]
                    out[3 * e + 2, m + 2 * S:m + H, :] += dl[1, q, 9 - e:9 - e + S, :]

        @pl.when(first)
        def _():
            for q in range(G):
                m = q * J * H
                pad[q, 0, 8:8 + H, :] = lh[p, 1, q].astype(F32)
                for e in range(3):
                    out[3 * e, m:m + S, :] += tl[1, q, 9 - e:9 - e + S, :]
                    out[6 + e, m + S:m + H, :] += pad[q, 0, 9 - e:9 - e + 2 * S, :]

    def apply(taps, k, dim):
        total = product(taps[0].astype(BF16), k[0, 0], 1, dim)
        for n in range(1, 9):
            total = total + product(taps[n].astype(BF16), k[n // 3, n % 3], 1, dim)
        return total

    def flat(src):
        return jnp.concatenate([src[q, j] for q in range(G) for j in range(J)], axis=0)

    def unflat(value, dst):
        for q in range(G):
            for j in range(J):
                m = (q * J + j) * H
                dst[q, j] = value[m:m + H]

    def channel_major(value, dst):
        for q in range(G):
            for j in range(J):
                m = (q * J + j) * H
                dst[:, q, j, :] = value[m:m + H].T.astype(BF16)

    per = C // 16
    blocks = acc.shape[1]

    def weight_terms(taps, cot, w):
        for n in range(9):
            term = product(taps[n], cot, 0, 0) * scale
            acc[w, n * per:(n + 1) * per] = term.reshape(per, 16, C)

    class Sum:
        def __init__(self, w, out):
            self.out, self.at, self.over = out, 0, False
            self.w, self.lo, self.length, self.done = w, 0, blocks, []
            self.used = [0, 0]
            self.sem = 0

        def members(self, bits):
            mine, place = [], 0
            for axis, s in bits:
                mine.append(lax.rem((t if axis == "tile" else f) // s, 2))
            found = []
            for k in range(1, 2 ** len(bits)):
                tile, face, digit = t, f, 0
                for pos, (axis, s) in enumerate(bits):
                    bit = mine[pos]
                    if (k >> pos) & 1:
                        if axis == "tile":
                            tile = tile + (1 - 2 * bit) * s
                        else:
                            face = face + (1 - 2 * bit) * s
                        bit = 1 - bit
                    digit = digit + bit * (1 << pos)
                found.append((digit, where_to(tile, face)))
            own = 0
            for pos, bit in enumerate(mine):
                own = own + bit * (1 << pos)
            return own, found

        def begin(self, n):
            bits, full = groups[n]
            own, found = self.members(bits)
            part = self.length // (len(found) + 1)
            w = self.w
            inbox = rfull if full else rlow
            at = self.used[full]
            self.flying = (inbox, at, part, len(found))
            for digit, dev in found:
                give = self.lo + digit * part
                if full:
                    out = acc.at[w, pl.ds(give, part)]
                else:
                    sbuf[w, pl.ds(give, part)] = acc[w, pl.ds(give, part)].astype(BF16)
                    out = sbuf.at[w, pl.ds(give, part)]
                at = self.used[full]
                self.used[full] += part
                remote(out, inbox.at[w, at:at + part], w_s.at[w, self.sem], w_r.at[w, self.sem], dev).start()
            keep = self.lo + own * part
            self.done.append((keep, part, found))
            self.lo, self.length = keep, part

        def end(self):
            inbox, at, part, count = self.flying
            whole = inbox.at[self.w, at:at + count * part]
            settle(whole, w_s.at[self.w, self.sem])
            settle(whole, w_r.at[self.w, self.sem])
            self.sem += 1
            total = acc[self.w, pl.ds(self.lo, self.length)]
            for n in range(count):
                total = total + inbox[self.w, at + n * part:at + (n + 1) * part].astype(F32)
            acc[self.w, pl.ds(self.lo, self.length)] = total

        def round(self):
            obuf[self.w, pl.ds(self.lo, self.length)] = acc[self.w, pl.ds(self.lo, self.length)].astype(BF16)

        def give(self, n):
            keep, part, found = self.done[n]
            self.flying = (part, len(found))
            for digit, dev in found:
                remote(obuf.at[self.w, pl.ds(keep, part)], obuf.at[self.w, pl.ds(keep, part)],
                       w_s.at[self.w, self.sem], w_r.at[self.w, self.sem], dev).start()

        def given(self):
            part, count = self.flying
            whole = obuf.at[self.w, 0:count * part]
            settle(whole, w_s.at[self.w, self.sem])
            settle(whole, w_r.at[self.w, self.sem])
            self.sem += 1

        def advance(self):
            at, count = self.at, len(groups)
            self.at += 1
            if at < count:
                if at > 0:
                    self.end()
                self.begin(at)
            elif at == count:
                self.end()
                self.round()
                self.give(count - 1)
            elif at < 2 * count:
                self.given()
                self.give(2 * count - 1 - at)
            elif at == 2 * count:
                self.given()
                for n in range(9):
                    self.out[n // 3, n % 3] = obuf[self.w, n * per:(n + 1) * per].reshape(C, C).astype(F32)
                self.over = True

    barrier = pltpu.get_barrier_semaphore()
    loads = [pltpu.make_async_copy(src, dst, in_s.at[n]) for n, (src, dst) in enumerate(
        ((fields_h, raw.at[0]), (upstream_h, raw.at[1]), (k1_h, k1), (k2_h, k2)))]
    for load in loads:
        load.start()

    @pl.loop(0, n_f)
    def _(df):
        @pl.loop(0, n_t)
        def _(dt):
            @pl.when(jnp.logical_or(df != f, dt != t))
            def _():
                pl.semaphore_signal(barrier, inc=1, device_id=where_to(dt, df), device_id_type=MESH)
    hidden, pre_grad = y.at[0], y.at[1]
    al[...] = jnp.zeros_like(al)
    tl[...] = jnp.zeros_like(tl)
    dl[...] = jnp.zeros_like(dl)
    for kind in range(2):
        loads[kind].wait()
        for q in range(G):
            for j in range(J):
                x[kind, q, j] = raw[kind, :, q, j, :].astype(F32).T.astype(BF16)
        stage(0, kind, x)
    if blocks > 9 * per:
        for w in range(2):
            acc[w, 9 * per:blocks] = jnp.zeros((blocks - 9 * per, 16, C), F32)
    pl.semaphore_wait(barrier, n_t * n_f - 1)

    start(0, x)
    loads[2].wait()
    loads[3].wait()
    await_arrivals(0, x)
    forward_taps(0, x.at[0], xf1)
    value, slope = gelu_parts(apply(xf1, k1, 0))
    unflat(value.astype(BF16), hidden)
    stage(1, 0, y)
    backward_taps(0, x.at[1], xb)
    cot = (apply(xb, k2, 1) * slope).astype(BF16)
    unflat(cot, pre_grad)
    stage(1, 1, y)
    start(1, y)
    one, two = Sum(0, w1_o), Sum(1, w2_o)
    cells = flat(hidden)
    for n in range(9):
        term = product(cells, xb[n].astype(BF16), 0, 0) * scale
        acc[1, n * per:(n + 1) * per] = term.reshape(per, 16, C)
    two.advance()
    weight_terms(xf1, cot, 0)
    one.advance()
    two.advance()
    one.advance()
    await_arrivals(1, y)
    forward_taps(1, hidden, xf2)
    channel_major(apply(xf2, k2, 0), res_o)
    two.advance()
    one.advance()
    backward_taps(1, pre_grad, xb)
    channel_major(apply(xb, k1, 1), fg_o)
    while not (one.over and two.over):
        one.advance()
        two.advance()
    await_sends(0, x)
    await_sends(1, y)


def deliver(*refs):
    sources, targets, sems = refs[0:4], refs[4:8], refs[8]
    moves = [pltpu.make_async_copy(a, b, sems.at[n]) for n, (a, b) in enumerate(zip(sources, targets))]
    for move in moves:
        move.start()
    for move in moves:
        move.wait()


def plan(n_t, n_f):
    tile_bits = [1 << i for i in range(n_t.bit_length() - 1)]
    face_bits = [1 << i for i in range(n_f.bit_length() - 1)]
    groups = [([("tile", tile_bits[0])], 1)]
    middle = [("face", s) for s in face_bits] + [("tile", s) for s in tile_bits[1:2]]
    rest = [("tile", s) for s in tile_bits[2:]]
    while middle:
        groups.append((middle[:2], 0))
        middle = middle[2:]
    while rest:
        groups.append((rest[:2], 0))
        rest = rest[2:]
    return groups


def run(fields, upstream, k1, k2, n_t, n_f):
    C, G, J, H = fields.shape
    S = H // 3
    E = J + 2
    M = G * J * H
    ranks = n_t * n_f
    blocks = -(-(9 * (C // 16)) // ranks) * ranks
    scale = 1.0 / (S * 12.0 ** 0.5)
    groups = plan(n_t, n_f)
    length, room = blocks, [1, 1]
    for bits, full in groups:
        others = 2 ** len(bits) - 1
        length //= others + 1
        room[full] += length * others
    dma = pltpu.SemaphoreType.DMA
    vmem = pl.BlockSpec(memory_space=pltpu.VMEM)
    hbm = pl.BlockSpec(memory_space=pltpu.HBM)
    held = [pltpu.with_memory_space_constraint(a, pltpu.HBM) for a in (fields, upstream, k1, k2)]
    return pl.pallas_call(
        functools.partial(body, n_t, n_f, scale, groups),
        out_shape=(
            jax.ShapeDtypeStruct((C, G, J, H), BF16),
            jax.ShapeDtypeStruct((C, G, J, H), BF16),
            jax.ShapeDtypeStruct((3, 3, C, C), F32),
            jax.ShapeDtypeStruct((3, 3, C, C), F32),
        ),
        in_specs=[hbm] * 4,
        out_specs=[vmem] * 4,
        scratch_shapes=[
            pltpu.VMEM((2, C, G, J, H), BF16),
            pltpu.VMEM((2, G, J, H, C), BF16),
            pltpu.VMEM(k1.shape, BF16),
            pltpu.VMEM(k2.shape, BF16),
            pltpu.VMEM((2, G, J, H, C), BF16),
            pltpu.VMEM((2, 2, 2, G, J, C), F32),
            pltpu.VMEM((2, 2, G, H, C), BF16),
            pltpu.VMEM((2, 2, G, H, C), BF16),
            pltpu.VMEM((2, 2, G, E, C), F32),
            pltpu.VMEM((2, 2, G, E, C), F32),
            pltpu.VMEM((2, n_t, 2, G, E, C), F32),
            pltpu.VMEM((2, n_t, 2, G, J, C), F32),
            pltpu.VMEM((2, n_t, 2, G, J, C), F32),
            pltpu.VMEM((2, G, S + 16, C), F32),
            pltpu.VMEM((2, G, S + 16, C), F32),
            pltpu.VMEM((2, G, S + 32, C), F32),
            pltpu.VMEM((G, J + 2, H + 16, C), F32),
            pltpu.VMEM((9, M, C), F32),
            pltpu.VMEM((9, M, C), BF16),
            pltpu.VMEM((9, M, C), BF16),
            pltpu.VMEM((2, blocks, 16, C), F32),
            pltpu.VMEM((2, blocks, 16, C), BF16),
            pltpu.VMEM((2, room[0], 16, C), BF16),
            pltpu.VMEM((2, room[1], 16, C), F32),
            pltpu.VMEM((2, blocks, 16, C), BF16),
            dma((2, 4)), dma((2, 4)),
            dma((2, 2)), dma((2, 2)), dma((2, 2)),
            dma((2, 2)), dma((2, 2)), dma((2, 2)),
            dma((2, 2 * len(groups))), dma((2, 2 * len(groups))), dma((4,)),
        ],
        compiler_params=pltpu.CompilerParams(
            collective_id=0, has_side_effects=True, vmem_limit_bytes=24 * 1024 * 1024),
    )(*held)


def send_out(made):
    vmem = pl.BlockSpec(memory_space=pltpu.VMEM)
    hbm = pl.BlockSpec(memory_space=pltpu.HBM)
    return pl.pallas_call(
        deliver,
        out_shape=[jax.ShapeDtypeStruct(a.shape, a.dtype) for a in made],
        in_specs=[vmem] * 4,
        out_specs=[hbm] * 4,
        scratch_shapes=[pltpu.SemaphoreType.DMA((4,))],
    )(*[pltpu.with_memory_space_constraint(a, pltpu.VMEM) for a in made])


def on_device(n_sub, n_t, n_f, fields, upstream, k1, k2):
    own = fields.shape[0]
    if n_sub > 1:
        fields = lax.all_gather(fields, "sub", axis=0, tiled=True)
        upstream = lax.all_gather(upstream, "sub", axis=0, tiled=True)
    made = run(fields, upstream, k1, k2, n_t, n_f)
    if n_sub > 1:
        at = lax.axis_index("sub") * own
        res, fgrad, w1, w2 = made
        return (
            lax.dynamic_slice_in_dim(res, at, own, 0),
            lax.dynamic_slice_in_dim(fgrad, at, own, 0),
            lax.dynamic_slice_in_dim(w1, at, own, 3),
            lax.dynamic_slice_in_dim(w2, at, own, 3),
        )
    return tuple(send_out(made))


def solution(mesh):
    placed = (P("sub", "face", "tile", "parts"), P("sub", "face", "tile", "parts"), P(), P())
    sizes = mesh.shape
    return jax.shard_map(
        functools.partial(on_device, sizes["sub"], sizes["tile"], sizes["face"]),
        mesh=mesh,
        in_specs=placed,
        out_specs=(
            P("sub", "face", "tile", "parts"),
            P("sub", "face", "tile", "parts"),
            P("parts", None, None, "sub"),
            P("parts", None, None, "sub"),
        ),
        check_vma=False,
    )
```

time: 44.5 us -> 35.4 us (0.80)
  Pallas kernels: 39.4 us -> 34.7 us
  local copies, waits for them, and re-layouts: 2.67 us -> 0 us
  other arithmetic: 1.59 us -> 0 us
    pallas_call x1, Pallas kernels: 39.4 us -> 33.6 us  [run(): pl.pallas_call(functools.partial(body, n_t, n_f, scale, groups), out_shap...]
    unnamed x6 -> x0, local copies, waits for them, and re-layouts: 2.67 us -> none
    reshape x2 -> x0, other arithmetic: 1.59 us -> none  [the longest x1 0.8 us: on_device(): w1.astype(F32).reshape(shape)]
    pallas_call x0 -> x1, Pallas kernels: none -> 1.01 us  [send_out(): pl.pallas_call(deliver, out_shape=[jax.ShapeDtypeStruct(a.shape, a.dtype)...]
where the time goes in v1:
time: 35.4 us; the launch traced here: 35.3 us
  Pallas kernels  34.7 us (98%)
  between operations  0.64 us (2%)
    pallas_call x1, Pallas kernels, run(): pl.pallas_call(functools.partial(body, n_t, n_f, scale, groups), out_shap...  33.6 us
    pallas_call x1, Pallas kernels, send_out(): pl.pallas_call(deliver, out_shape=[jax.ShapeDtypeStruct(a.shape, a.dtype)...  1.01 us

profile of v1, /device:TPU:0, one launch (start us, length us, event | category | flops | bytes accessed | tf_op | source)
XLA Modules:
  0.0 35.3 jit_solution(13984539708578472627)
XLA Ops:
  0.6 33.6 %shard_map.75 = (bf16[96,2,2,96]{3,2,1,0:T(2,128)(2,1)S(1)}, bf16[96,2,2,96]{3,2,1,0:T(2,128)(2,1)S(1)}, f32[3,3,96,96]{3,2,1,0:T(8,128)S(1)}, f32[3,3,96,96]{3,2,1,0:T(8,128)S(1)}) custom-call(bf16[96,2,2,96]{3,2,1,0:T(2,128)(2,1)} %fields_h.1, bf16[96,2,2,96]{3,2,1,0:T(2,128)(2,1)} %upstream_h.1, bf16[3,3,96,96]{3,2,1,0:T(8,128)(2,1)} %k1_h.1, ...), custom_call_target="tpu_custom_call" | custom-call | tf_op jit(solution)/shard_map/pallas_call | solution.py:535
  34.3 1.0 %shard_map.76 = (bf16[96,2,2,96]{3,2,1,0:T(2,128)(2,1)}, bf16[96,2,2,96]{3,2,1,0:T(2,128)(2,1)}, f32[3,3,96,96]{3,2,1,0:T(8,128)}, f32[3,3,96,96]{3,2,1,0:T(8,128)}) custom-call(bf16[96,2,2,96]{3,2,1,0:T(2,128)(2,1)S(1)} %get-tuple-element.8.refs_0_, bf16[96,2,2,96]{3,2,1,0:T(2,128)(2,1)S(1)} %get-tuple-element.9.refs_1_, ...), custom_call_target="tpu_custom_call" | custom-call | tf_op jit(solution)/shard_map/pallas_call | solution.py:584

commit v2 on v1

--- a/solution.py
+++ b/solution.py
@@ -10,6 +10,7 @@
 MESH = pl.DeviceIdType.MESH
 F32 = jnp.float32
 BF16 = jnp.bfloat16
+LANES = 128
 
 
 def gelu_parts(v):
@@ -319,12 +320,20 @@
                 dst[:, q, j, :] = value[m:m + H].T.astype(BF16)
 
     per = C // 16
+    tiles = -(-9 * C // LANES)
     blocks = acc.shape[1]
 
-    def weight_terms(taps, cot, w):
+    def pack(terms, w):
+        spare = tiles * LANES - 9 * C
+        wide = jnp.concatenate(terms + ([jnp.zeros((C, spare), F32)] if spare else []), axis=1)
+        for n in range(tiles):
+            acc[w, n * per:(n + 1) * per] = wide[:, n * LANES:(n + 1) * LANES].reshape(per, 16, LANES)
+
+    def unpack(w, out):
+        parts = [obuf[w, n * per:(n + 1) * per].astype(F32).reshape(C, LANES) for n in range(tiles)]
+        wide = jnp.concatenate(parts, axis=1)
         for n in range(9):
-            term = product(taps[n], cot, 0, 0) * scale
-            acc[w, n * per:(n + 1) * per] = term.reshape(per, 16, C)
+            out[n // 3, n % 3] = wide[:, n * C:(n + 1) * C]
 
     class Sum:
         def __init__(self, w, out):
@@ -334,7 +343,7 @@
             self.sem = 0
 
         def members(self, bits):
-            mine, place = [], 0
+            mine = []
             for axis, s in bits:
                 mine.append(lax.rem((t if axis == "tile" else f) // s, 2))
             found = []
@@ -356,13 +365,22 @@
             return own, found
 
         def begin(self, n):
-            bits, full = groups[n]
+            bits, full, whole = groups[n]
             own, found = self.members(bits)
-            part = self.length // (len(found) + 1)
             w = self.w
             inbox = rfull if full else rlow
             at = self.used[full]
-            self.flying = (inbox, at, part, len(found))
+            part = self.length if whole else self.length // (len(found) + 1)
+            self.flying = (inbox, at, part, len(found), whole)
+            if whole:
+                piece = pl.ds(self.lo, part)
+                mine = pl.ds(at + own * part, part)
+                sbuf[w, piece] = acc[w, piece].astype(BF16)
+                for digit, dev in found:
+                    remote(sbuf.at[w, piece], inbox.at[w, mine], w_s.at[w, self.sem], w_r.at[w, self.sem], dev).start()
+                inbox[w, mine] = sbuf[w, piece]
+                self.used[full] += part * (len(found) + 1)
+                return
             for digit, dev in found:
                 give = self.lo + digit * part
                 if full:
@@ -378,21 +396,22 @@
             self.lo, self.length = keep, part
 
         def end(self):
-            inbox, at, part, count = self.flying
-            whole = inbox.at[self.w, at:at + count * part]
-            settle(whole, w_s.at[self.w, self.sem])
-            settle(whole, w_r.at[self.w, self.sem])
+            inbox, at, part, count, whole = self.flying
+            sent = inbox.at[self.w, at:at + count * part]
+            settle(sent, w_s.at[self.w, self.sem])
+            settle(sent, w_r.at[self.w, self.sem])
             self.sem += 1
-            total = acc[self.w, pl.ds(self.lo, self.length)]
-            for n in range(count):
-                total = total + inbox[self.w, at + n * part:at + (n + 1) * part].astype(F32)
+            terms = [inbox[self.w, at + n * part:at + (n + 1) * part].astype(F32) for n in range(count + whole)]
+            total = terms.pop(0) if whole else acc[self.w, pl.ds(self.lo, self.length)]
+            for term in terms:
+                total = total + term
             acc[self.w, pl.ds(self.lo, self.length)] = total
 
         def round(self):
             obuf[self.w, pl.ds(self.lo, self.length)] = acc[self.w, pl.ds(self.lo, self.length)].astype(BF16)
 
-        def give(self, n):
-            keep, part, found = self.done[n]
+        def give(self):
+            keep, part, found = self.done.pop()
             self.flying = (part, len(found))
             for digit, dev in found:
                 remote(obuf.at[self.w, pl.ds(keep, part)], obuf.at[self.w, pl.ds(keep, part)],
@@ -408,21 +427,22 @@
         def advance(self):
             at, count = self.at, len(groups)
             self.at += 1
+            if self.over:
+                return
             if at < count:
                 if at > 0:
                     self.end()
                 self.begin(at)
-            elif at == count:
+                return
+            if at == count:
                 self.end()
                 self.round()
-                self.give(count - 1)
-            elif at < 2 * count:
+            else:
                 self.given()
-                self.give(2 * count - 1 - at)
-            elif at == 2 * count:
-                self.given()
-                for n in range(9):
-                    self.out[n // 3, n % 3] = obuf[self.w, n * per:(n + 1) * per].reshape(C, C).astype(F32)
+            if self.done:
+                self.give()
+            else:
+                unpack(self.w, self.out)
                 self.over = True
 
     barrier = pltpu.get_barrier_semaphore()
@@ -448,9 +468,9 @@
             for j in range(J):
                 x[kind, q, j] = raw[kind, :, q, j, :].astype(F32).T.astype(BF16)
         stage(0, kind, x)
-    if blocks > 9 * per:
+    if blocks > tiles * per:
         for w in range(2):
-            acc[w, 9 * per:blocks] = jnp.zeros((blocks - 9 * per, 16, C), F32)
+            acc[w, tiles * per:blocks] = jnp.zeros((blocks - tiles * per, 16, LANES), F32)
     pl.semaphore_wait(barrier, n_t * n_f - 1)
 
     start(0, x)
@@ -468,11 +488,11 @@
     start(1, y)
     one, two = Sum(0, w1_o), Sum(1, w2_o)
     cells = flat(hidden)
-    for n in range(9):
-        term = product(cells, xb[n].astype(BF16), 0, 0) * scale
-        acc[1, n * per:(n + 1) * per] = term.reshape(per, 16, C)
+    pack([product(cells, xb[n].astype(BF16), 0, 0) * scale for n in range(9)], 1)
     two.advance()
-    weight_terms(xf1, cot, 0)
+    pack([product(xf1[n], cot, 0, 0) * scale for n in range(9)], 0)
+    one.advance()
+    two.advance()
     one.advance()
     two.advance()
     one.advance()
@@ -500,17 +520,18 @@
 
 
 def plan(n_t, n_f):
-    tile_bits = [1 << i for i in range(n_t.bit_length() - 1)]
-    face_bits = [1 << i for i in range(n_f.bit_length() - 1)]
-    groups = [([("tile", tile_bits[0])], 1)]
-    middle = [("face", s) for s in face_bits] + [("tile", s) for s in tile_bits[1:2]]
-    rest = [("tile", s) for s in tile_bits[2:]]
+    tile_bits = [("tile", 1 << i) for i in range(n_t.bit_length() - 1)]
+    face_bits = [("face", 1 << i) for i in range(n_f.bit_length() - 1)]
+    groups = [(tile_bits[:1], 1, 0)]
+    middle, rest = face_bits + tile_bits[1:3], tile_bits[3:]
     while middle:
-        groups.append((middle[:2], 0))
-        middle = middle[2:]
-    while rest:
-        groups.append((rest[:2], 0))
+        groups.append((middle[:3], 0, 0))
+        middle = middle[3:]
+    while len(rest) > 2:
+        groups.append((rest[:2], 0, 0))
         rest = rest[2:]
+    if rest:
+        groups.append((rest, 0, 1))
     return groups
 
 
@@ -519,15 +540,22 @@
     S = H // 3
     E = J + 2
     M = G * J * H
-    ranks = n_t * n_f
-    blocks = -(-(9 * (C // 16)) // ranks) * ranks
     scale = 1.0 / (S * 12.0 ** 0.5)
     groups = plan(n_t, n_f)
+    cuts, stages = 1, 0
+    for bits, full, whole in groups:
+        cuts *= 1 if whole else 2 ** len(bits)
+        stages += 1 if whole else 2
+    blocks = -(-9 * C // LANES) * (C // 16)
+    blocks = -(-blocks // cuts) * cuts
     length, room = blocks, [1, 1]
-    for bits, full in groups:
-        others = 2 ** len(bits) - 1
-        length //= others + 1
-        room[full] += length * others
+    for bits, full, whole in groups:
+        members = 2 ** len(bits)
+        if whole:
+            room[full] += length * members
+        else:
+            length //= members
+            room[full] += length * (members - 1)
     dma = pltpu.SemaphoreType.DMA
     vmem = pl.BlockSpec(memory_space=pltpu.VMEM)
     hbm = pl.BlockSpec(memory_space=pltpu.HBM)
@@ -563,15 +591,15 @@
             pltpu.VMEM((9, M, C), F32),
             pltpu.VMEM((9, M, C), BF16),
             pltpu.VMEM((9, M, C), BF16),
-            pltpu.VMEM((2, blocks, 16, C), F32),
-            pltpu.VMEM((2, blocks, 16, C), BF16),
-            pltpu.VMEM((2, room[0], 16, C), BF16),
-            pltpu.VMEM((2, room[1], 16, C), F32),
-            pltpu.VMEM((2, blocks, 16, C), BF16),
+            pltpu.VMEM((2, blocks, 16, LANES), F32),
+            pltpu.VMEM((2, blocks, 16, LANES), BF16),
+            pltpu.VMEM((2, room[0], 16, LANES), BF16),
+            pltpu.VMEM((2, room[1], 16, LANES), F32),
+            pltpu.VMEM((2, blocks, 16, LANES), BF16),
             dma((2, 4)), dma((2, 4)),
             dma((2, 2)), dma((2, 2)), dma((2, 2)),
             dma((2, 2)), dma((2, 2)), dma((2, 2)),
-            dma((2, 2 * len(groups))), dma((2, 2 * len(groups))), dma((4,)),
+            dma((2, stages)), dma((2, stages)), dma((4,)),
         ],
         compiler_params=pltpu.CompilerParams(
             collective_id=0, has_side_effects=True, vmem_limit_bytes=24 * 1024 * 1024),

time: 35.4 us -> 31.2 us (0.88)
  Pallas kernels: 34.7 us -> 30.4 us
    pallas_call x1, Pallas kernels: 33.6 us -> 29.4 us  [run(): pl.pallas_call(functools.partial(body, n_t, n_f, scale, groups), out_shap...]
where the time goes in v2:
time: 31.2 us; the launch traced here: 31.1 us
  Pallas kernels  30.4 us (97%)
  between operations  0.64 us (2%)
    pallas_call x1, Pallas kernels, run(): pl.pallas_call(functools.partial(body, n_t, n_f, scale, groups), out_shap...  29.4 us
    pallas_call x1, Pallas kernels, send_out(): pl.pallas_call(deliver, out_shape=[jax.ShapeDtypeStruct(a.shape, a.dtype)...  1.01 us

profile of v2, /device:TPU:0, one launch (start us, length us, event | category | flops | bytes accessed | tf_op | source)
XLA Modules:
  0.0 31.1 jit_solution(18341912614474031886)
XLA Ops:
  0.6 29.4 %shard_map.75 = (bf16[96,2,2,96]{3,2,1,0:T(2,128)(2,1)S(1)}, bf16[96,2,2,96]{3,2,1,0:T(2,128)(2,1)S(1)}, f32[3,3,96,96]{3,2,1,0:T(8,128)S(1)}, f32[3,3,96,96]{3,2,1,0:T(8,128)S(1)}) custom-call(bf16[96,2,2,96]{3,2,1,0:T(2,128)(2,1)} %fields_h.1, bf16[96,2,2,96]{3,2,1,0:T(2,128)(2,1)} %upstream_h.1, bf16[3,3,96,96]{3,2,1,0:T(8,128)(2,1)} %k1_h.1, ...), custom_call_target="tpu_custom_call" | custom-call | tf_op jit(solution)/shard_map/pallas_call | solution.py:563
  30.1 1.0 %shard_map.76 = (bf16[96,2,2,96]{3,2,1,0:T(2,128)(2,1)}, bf16[96,2,2,96]{3,2,1,0:T(2,128)(2,1)}, f32[3,3,96,96]{3,2,1,0:T(8,128)}, f32[3,3,96,96]{3,2,1,0:T(8,128)}) custom-call(bf16[96,2,2,96]{3,2,1,0:T(2,128)(2,1)S(1)} %get-tuple-element.8.refs_0_, bf16[96,2,2,96]{3,2,1,0:T(2,128)(2,1)S(1)} %get-tuple-element.9.refs_1_, ...), custom_call_target="tpu_custom_call" | custom-call | tf_op jit(solution)/shard_map/pallas_call | solution.py:612

commit v3 on v2

--- a/solution.py
+++ b/solution.py
@@ -27,7 +27,7 @@
 
 
 def body(n_t, n_f, scale, groups, fields_h, upstream_h, k1_h, k2_h, res_o, fg_o, w1_o, w2_o,
-         raw, x, k1, k2, y, rows, lh, rh, ap, bm, aps, tr, dr, tl, dl, al, pad, xb, xf1, xf2,
+         raw, x, k1, k2, y, rows, lh, rh, ap, bm, aps, tr, dr, tl, dl, al, pad, xb, xf1, xf2, pre, back,
          acc, sbuf, rlow, rfull, obuf,
          col_s, col_r, line_s, a_r, b_r, t_s, d_s, row_r, w_s, w_r, in_s):
     _, G, J, H, C = x.shape
@@ -42,6 +42,8 @@
     inner_left = jnp.logical_not(first)
     inner_right = jnp.logical_not(last)
 
+    upper, lower = slice(S - 16, H), slice(0, 2 * S + 16)
+
     def where_to(tile, face):
         return {"tile": tile, "face": face}
 
@@ -58,10 +60,10 @@
         left = lambda: remote(c0, rh.at[p], col_s.at[p, 1], col_r.at[p, 1], where_to(jnp.maximum(t - 1, 0), f))
         seam = []
         if G > 1:
-            seam.append((first, lambda: remote(src.at[:, 1:G, 0], rh.at[p, :, 0:G - 1], col_s.at[p, 2], col_r.at[p, 2], where_to(n_t - 1, f))))
-            seam.append((last, lambda: remote(src.at[:, 0:G - 1, J - 1], lh.at[p, :, 1:G], col_s.at[p, 2], col_r.at[p, 2], where_to(0, f))))
-        seam.append((first, lambda: remote(src.at[:, 0:1, 0], rh.at[p, :, G - 1:G], col_s.at[p, 3], col_r.at[p, 3], where_to(n_t - 1, fp))))
-        seam.append((last, lambda: remote(src.at[:, G - 1:G, J - 1], lh.at[p, :, 0:1], col_s.at[p, 3], col_r.at[p, 3], where_to(0, fn))))
+            seam.append((first, lambda: remote(src.at[:, 1:G, 0, upper], rh.at[p, :, 0:G - 1, upper], col_s.at[p, 2], col_r.at[p, 2], where_to(n_t - 1, f))))
+            seam.append((last, lambda: remote(src.at[:, 0:G - 1, J - 1, lower], lh.at[p, :, 1:G, lower], col_s.at[p, 2], col_r.at[p, 2], where_to(0, f))))
+        seam.append((first, lambda: remote(src.at[:, 0:1, 0, upper], rh.at[p, :, G - 1:G, upper], col_s.at[p, 3], col_r.at[p, 3], where_to(n_t - 1, fp))))
+        seam.append((last, lambda: remote(src.at[:, G - 1:G, J - 1, lower], lh.at[p, :, 0:1, lower], col_s.at[p, 3], col_r.at[p, 3], where_to(0, fn))))
         a_own = lambda d: remote(aps.at[p, d, :, 1:G], ap.at[p, :, 0:G - 1], line_s.at[p, 0], a_r.at[p, 0], where_to(d, f))
         a_oth = lambda d: remote(aps.at[p, d, :, 0:1], ap.at[p, :, G - 1:G], line_s.at[p, 1], a_r.at[p, 1], where_to(d, fp))
         b_own = lambda d: remote(aps.at[p, d, :, 0:G - 1], bm.at[p, :, 1:G], line_s.at[p, 0], b_r.at[p, 0], where_to(d, f))
@@ -95,20 +97,6 @@
 
     def start(p, src):
         right, left, seam, a_own, a_oth, b_own, b_oth, t_own, t_oth, d_own, d_oth = copies(p, src)
-        t_oth(t).start()
-        d_oth(t).start()
-        if G > 1:
-            @pl.when(inner_left)
-            def _():
-                t_own(t).start()
-
-            @pl.when(inner_right)
-            def _():
-                d_own(t).start()
-        for cond, make in seam:
-            @pl.when(cond)
-            def _(make=make):
-                make().start()
 
         @pl.when(first)
         def _():
@@ -134,6 +122,21 @@
                 bm[p, :, 1:G] = aps[p, n_t - 1, :, 0:G - 1]
                 dr[p, n_t - 1, :, 0:G - 1] = rows[p, 1, :, 1:G]
 
+        for cond, make in seam:
+            @pl.when(cond)
+            def _(make=make):
+                make().start()
+        t_oth(t).start()
+        d_oth(t).start()
+        if G > 1:
+            @pl.when(inner_left)
+            def _():
+                t_own(t).start()
+
+            @pl.when(inner_right)
+            def _():
+                d_own(t).start()
+
         @pl.when(inner_right)
         def _():
             right().start()
@@ -157,13 +160,15 @@
             if G > 1:
                 b_own(0).wait_recv()
 
+        a_oth(0).wait_recv()
+        b_oth(0).wait_recv()
+
+    def await_seam(p, src):
+        seam = copies(p, src)[2]
         for cond, make in seam:
             @pl.when(last if cond is first else first)
             def _(make=make):
                 make().wait_recv()
-
-        a_oth(0).wait_recv()
-        b_oth(0).wait_recv()
 
         @pl.when(first)
         def _():
@@ -214,26 +219,33 @@
             for j in range(J):
                 pad[q, 1 + j, 8:8 + H, :] = src[q, j].astype(F32)
 
-    def forward_taps(p, src, out):
+    def forward_taps(p, src, out, late):
         fill_columns(src)
         for q in range(G):
             @pl.when(inner_left)
             def _():
                 pad[q, 0, 8:8 + H, :] = lh[p, 0, q].astype(F32)
 
-            @pl.when(first)
-            def _():
-                pad[q, 0, 8:8 + S, :] = tl[0, q, 8:8 + S, :]
-                pad[q, 0, 8 + S:8 + H, :] = lh[p, 0, q, 0:2 * S].astype(F32)
-
             @pl.when(inner_right)
             def _():
                 pad[q, J + 1, 8:8 + H, :] = rh[p, 0, q].astype(F32)
 
-            @pl.when(last)
-            def _():
-                pad[q, J + 1, 8:8 + 2 * S, :] = rh[p, 0, q, S:H].astype(F32)
-                pad[q, J + 1, 8 + 2 * S:8 + H, :] = dl[0, q, 8:8 + S, :]
+            if late:
+                @pl.when(first)
+                def _():
+                    pad[q, 0, 8:8 + H, :] = jnp.zeros((H, C), F32)
+
+                @pl.when(last)
+                def _():
+                    pad[q, J + 1, 8:8 + H, :] = jnp.zeros((H, C), F32)
+            else:
+                @pl.when(first)
+                def _():
+                    forward_edge(p, q, 0)
+
+                @pl.when(last)
+                def _():
+                    forward_edge(p, q, J + 1)
             for j in range(E):
                 pad[q, j, 7:8, :] = ap[p, 0, q, j:j + 1]
                 pad[q, j, 8 + H:9 + H, :] = bm[p, 0, q, j:j + 1]
@@ -244,7 +256,31 @@
                         m = (q * J + j) * H
                         out[3 * a + b, m:m + H, :] = pad[q, j + a, 7 + b:7 + b + H, :].astype(BF16)
 
-    def backward_taps(p, src, out):
+    def forward_edge(p, q, j):
+        if j == 0:
+            pad[q, 0, 8:8 + S, :] = tl[0, q, 8:8 + S, :]
+            pad[q, 0, 8 + S:8 + H, :] = lh[p, 0, q, 0:2 * S].astype(F32)
+        else:
+            pad[q, J + 1, 8:8 + 2 * S, :] = rh[p, 0, q, S:H].astype(F32)
+            pad[q, J + 1, 8 + 2 * S:8 + H, :] = dl[0, q, 8:8 + S, :]
+
+    def forward_late(p, out, k, total):
+        for cond, a, j in ((first, 0, 0), (last, 2, J + 1)):
+            @pl.when(cond)
+            def _(a=a, j=j):
+                for q in range(G):
+                    forward_edge(p, q, j)
+                    pad[q, j, 7:8, :] = jnp.zeros((1, C), F32)
+                    pad[q, j, 8 + H:9 + H, :] = jnp.zeros((1, C), F32)
+                    m = (q * J + j - a) * H
+                    more = total[m:m + H, :]
+                    for b in range(3):
+                        tap = pad[q, j, 7 + b:7 + b + H, :].astype(BF16)
+                        more = more + product(tap, k[a, b], 1, 0)
+                        out[3 * a + b, m:m + H, :] += tap
+                    total[m:m + H, :] = more
+
+    def backward_taps(p, src, out, late):
         fill_columns(src)
         for q in range(G):
             @pl.when(inner_left)
@@ -279,24 +315,35 @@
                     m = (q * J + j) * H
                     out[b, m:m + 1, :] += top[j + 2 - b:j + 3 - b]
                     out[6 + b, m + H - 1:m + H, :] += low[j + 2 - b:j + 3 - b]
+        if not late:
+            backward_late(p, out, None, None)
+
+    def backward_late(p, out, k, total):
+        def add(n, m, rows_at, value):
+            out[n, m + rows_at.start:m + rows_at.stop, :] += value
+            if total is not None:
+                here = slice(m + rows_at.start, m + rows_at.stop)
+                total[here, :] += product(value.astype(BF16), k[n // 3, n % 3], 1, 1)
 
         @pl.when(last)
         def _():
             for q in range(G):
                 m = (q * J + J - 1) * H
                 pad[q, J + 1, 8:8 + H, :] = rh[p, 1, q].astype(F32)
+                pad[q, J + 1, 8 + H:9 + H, :] = jnp.zeros((1, C), F32)
                 for e in range(3):
-                    out[e, m:m + 2 * S, :] += pad[q, J + 1, 8 + S + 1 - e:8 + H + 1 - e, :]
-                    out[3 * e + 2, m + 2 * S:m + H, :] += dl[1, q, 9 - e:9 - e + S, :]
+                    add(e, m, slice(0, 2 * S), pad[q, J + 1, 8 + S + 1 - e:8 + H + 1 - e, :])
+                    add(3 * e + 2, m, slice(2 * S, H), dl[1, q, 9 - e:9 - e + S, :])
 
         @pl.when(first)
         def _():
             for q in range(G):
                 m = q * J * H
+                pad[q, 0, 7:8, :] = jnp.zeros((1, C), F32)
                 pad[q, 0, 8:8 + H, :] = lh[p, 1, q].astype(F32)
                 for e in range(3):
-                    out[3 * e, m:m + S, :] += tl[1, q, 9 - e:9 - e + S, :]
-                    out[6 + e, m + S:m + H, :] += pad[q, 0, 9 - e:9 - e + 2 * S, :]
+                    add(3 * e, m, slice(0, S), tl[1, q, 9 - e:9 - e + S, :])
+                    add(6 + e, m, slice(S, H), pad[q, 0, 9 - e:9 - e + 2 * S, :])
 
     def apply(taps, k, dim):
         total = product(taps[0].astype(BF16), k[0, 0], 1, dim)
@@ -347,7 +394,7 @@
             for axis, s in bits:
                 mine.append(lax.rem((t if axis == "tile" else f) // s, 2))
             found = []
-            for k in range(1, 2 ** len(bits)):
+            for k in reversed(range(1, 2 ** len(bits))):
                 tile, face, digit = t, f, 0
                 for pos, (axis, s) in enumerate(bits):
                     bit = mine[pos]
@@ -477,15 +524,17 @@
     loads[2].wait()
     loads[3].wait()
     await_arrivals(0, x)
-    forward_taps(0, x.at[0], xf1)
-    value, slope = gelu_parts(apply(xf1, k1, 0))
+    forward_taps(0, x.at[0], xf1, True)
+    pre[...] = apply(xf1, k1, 0)
+    backward_taps(0, x.at[1], xb, True)
+    back[...] = apply(xb, k2, 1)
+    await_seam(0, x)
+    forward_late(0, xf1, k1, pre)
+    backward_late(0, xb, k2, back)
+    value, slope = gelu_parts(pre[...])
     unflat(value.astype(BF16), hidden)
-    stage(1, 0, y)
-    backward_taps(0, x.at[1], xb)
-    cot = (apply(xb, k2, 1) * slope).astype(BF16)
+    cot = (back[...] * slope).astype(BF16)
     unflat(cot, pre_grad)
-    stage(1, 1, y)
-    start(1, y)
     one, two = Sum(0, w1_o), Sum(1, w2_o)
     cells = flat(hidden)
     pack([product(cells, xb[n].astype(BF16), 0, 0) * scale for n in range(9)], 1)
@@ -494,18 +543,22 @@
     one.advance()
     two.advance()
     one.advance()
+    stage(1, 0, y)
+    stage(1, 1, y)
+    start(1, y)
+    two.advance()
+    one.advance()
     two.advance()
     one.advance()
     await_arrivals(1, y)
-    forward_taps(1, hidden, xf2)
+    await_seam(1, y)
+    forward_taps(1, hidden, xf2, False)
     channel_major(apply(xf2, k2, 0), res_o)
-    two.advance()
-    one.advance()
-    backward_taps(1, pre_grad, xb)
+    backward_taps(1, pre_grad, xb, False)
     channel_major(apply(xb, k1, 1), fg_o)
     while not (one.over and two.over):
+        two.advance()
         one.advance()
-        two.advance()
     await_sends(0, x)
     await_sends(1, y)
 
@@ -591,6 +644,8 @@
             pltpu.VMEM((9, M, C), F32),
             pltpu.VMEM((9, M, C), BF16),
             pltpu.VMEM((9, M, C), BF16),
+            pltpu.VMEM((M, C), F32),
+            pltpu.VMEM((M, C), F32),
             pltpu.VMEM((2, blocks, 16, LANES), F32),
             pltpu.VMEM((2, blocks, 16, LANES), BF16),
             pltpu.VMEM((2, room[0], 16, LANES), BF16),

time: 31.2 us -> 30.4 us (0.974)
  Pallas kernels: 30.4 us -> 29.6 us
    pallas_call x1, Pallas kernels: 29.4 us -> 28.6 us  [run(): pl.pallas_call(functools.partial(body, n_t, n_f, scale, groups), out_shap...]
where the time goes in v3:
time: 30.4 us; the launch traced here: 30.3 us
  Pallas kernels  29.6 us (97%)
  between operations  0.64 us (2%)
    pallas_call x1, Pallas kernels, run(): pl.pallas_call(functools.partial(body, n_t, n_f, scale, groups), out_shap...  28.6 us
    pallas_call x1, Pallas kernels, send_out(): pl.pallas_call(deliver, out_shape=[jax.ShapeDtypeStruct(a.shape, a.dtype)...  1.01 us

profile of v3, /device:TPU:0, one launch (start us, length us, event | category | flops | bytes accessed | tf_op | source)
XLA Modules:
  0.0 30.3 jit_solution(17404612211371151795)
XLA Ops:
  0.6 28.6 %shard_map.75 = (bf16[96,2,2,96]{3,2,1,0:T(2,128)(2,1)S(1)}, bf16[96,2,2,96]{3,2,1,0:T(2,128)(2,1)S(1)}, f32[3,3,96,96]{3,2,1,0:T(8,128)S(1)}, f32[3,3,96,96]{3,2,1,0:T(8,128)S(1)}) custom-call(bf16[96,2,2,96]{3,2,1,0:T(2,128)(2,1)} %fields_h.1, bf16[96,2,2,96]{3,2,1,0:T(2,128)(2,1)} %upstream_h.1, bf16[3,3,96,96]{3,2,1,0:T(8,128)(2,1)} %k1_h.1, ...), custom_call_target="tpu_custom_call" | custom-call | tf_op jit(solution)/shard_map/pallas_call | solution.py:616
  29.3 1.0 %shard_map.76 = (bf16[96,2,2,96]{3,2,1,0:T(2,128)(2,1)}, bf16[96,2,2,96]{3,2,1,0:T(2,128)(2,1)}, f32[3,3,96,96]{3,2,1,0:T(8,128)}, f32[3,3,96,96]{3,2,1,0:T(8,128)}) custom-call(bf16[96,2,2,96]{3,2,1,0:T(2,128)(2,1)S(1)} %get-tuple-element.8.refs_0_, bf16[96,2,2,96]{3,2,1,0:T(2,128)(2,1)S(1)} %get-tuple-element.9.refs_1_, ...), custom_call_target="tpu_custom_call" | custom-call | tf_op jit(solution)/shard_map/pallas_call | solution.py:667

commit v4 on v3

--- a/solution.py
+++ b/solution.py
@@ -27,12 +27,13 @@
 
 
 def body(n_t, n_f, scale, groups, fields_h, upstream_h, k1_h, k2_h, res_o, fg_o, w1_o, w2_o,
-         raw, x, k1, k2, y, rows, lh, rh, ap, bm, aps, tr, dr, tl, dl, al, pad, xb, xf1, xf2, pre, back,
+         raw, x, k1, k2, y, rows, lh, rh, ap, bm, aps, tr, dr, tl, dl, al, pad, xb, xf1, xf2, xc, kf, kb, pre, back,
          acc, sbuf, rlow, rfull, obuf,
-         col_s, col_r, line_s, a_r, b_r, t_s, d_s, row_r, w_s, w_r, in_s):
+         col_s, col_r, line_s, a_r, b_r, t_s, d_s, row_r, w_s, w_r):
     _, G, J, H, C = x.shape
     S = H // 3
     E = J + 2
+    W = xc.shape[1] // 9
     t = lax.axis_index("tile")
     f = lax.axis_index("face")
     fn = lax.rem(f + 1, n_f)
@@ -56,22 +57,22 @@
 
     def copies(p, src):
         c0, cl = src.at[:, :, 0], src.at[:, :, J - 1]
-        right = lambda: remote(cl, lh.at[p], col_s.at[p, 0], col_r.at[p, 0], where_to(jnp.minimum(t + 1, n_t - 1), f))
-        left = lambda: remote(c0, rh.at[p], col_s.at[p, 1], col_r.at[p, 1], where_to(jnp.maximum(t - 1, 0), f))
+        right = lambda: remote(cl, lh.at[p], col_s.at[0], col_r.at[p, 0], where_to(jnp.minimum(t + 1, n_t - 1), f))
+        left = lambda: remote(c0, rh.at[p], col_s.at[1], col_r.at[p, 1], where_to(jnp.maximum(t - 1, 0), f))
         seam = []
         if G > 1:
-            seam.append((first, lambda: remote(src.at[:, 1:G, 0, upper], rh.at[p, :, 0:G - 1, upper], col_s.at[p, 2], col_r.at[p, 2], where_to(n_t - 1, f))))
-            seam.append((last, lambda: remote(src.at[:, 0:G - 1, J - 1, lower], lh.at[p, :, 1:G, lower], col_s.at[p, 2], col_r.at[p, 2], where_to(0, f))))
-        seam.append((first, lambda: remote(src.at[:, 0:1, 0, upper], rh.at[p, :, G - 1:G, upper], col_s.at[p, 3], col_r.at[p, 3], where_to(n_t - 1, fp))))
-        seam.append((last, lambda: remote(src.at[:, G - 1:G, J - 1, lower], lh.at[p, :, 0:1, lower], col_s.at[p, 3], col_r.at[p, 3], where_to(0, fn))))
-        a_own = lambda d: remote(aps.at[p, d, :, 1:G], ap.at[p, :, 0:G - 1], line_s.at[p, 0], a_r.at[p, 0], where_to(d, f))
-        a_oth = lambda d: remote(aps.at[p, d, :, 0:1], ap.at[p, :, G - 1:G], line_s.at[p, 1], a_r.at[p, 1], where_to(d, fp))
-        b_own = lambda d: remote(aps.at[p, d, :, 0:G - 1], bm.at[p, :, 1:G], line_s.at[p, 0], b_r.at[p, 0], where_to(d, f))
-        b_oth = lambda d: remote(aps.at[p, d, :, G - 1:G], bm.at[p, :, 0:1], line_s.at[p, 1], b_r.at[p, 1], where_to(d, fn))
-        t_own = lambda d: remote(rows.at[p, 0, :, 0:G - 1], tr.at[p, d, :, 1:G], t_s.at[p, 0], row_r.at[p, 0], where_to(0, f))
-        t_oth = lambda d: remote(rows.at[p, 0, :, G - 1:G], tr.at[p, d, :, 0:1], t_s.at[p, 1], row_r.at[p, 1], where_to(0, fn))
-        d_own = lambda d: remote(rows.at[p, 1, :, 1:G], dr.at[p, d, :, 0:G - 1], d_s.at[p, 0], row_r.at[p, 0], where_to(n_t - 1, f))
-        d_oth = lambda d: remote(rows.at[p, 1, :, 0:1], dr.at[p, d, :, G - 1:G], d_s.at[p, 1], row_r.at[p, 1], where_to(n_t - 1, fp))
+            seam.append((first, lambda: remote(src.at[:, 1:G, 0, upper], rh.at[p, :, 0:G - 1, upper], col_s.at[1], col_r.at[p, 1], where_to(n_t - 1, f))))
+            seam.append((last, lambda: remote(src.at[:, 0:G - 1, J - 1, lower], lh.at[p, :, 1:G, lower], col_s.at[0], col_r.at[p, 0], where_to(0, f))))
+        seam.append((first, lambda: remote(src.at[:, 0:1, 0, upper], rh.at[p, :, G - 1:G, upper], col_s.at[1], col_r.at[p, 1], where_to(n_t - 1, fp))))
+        seam.append((last, lambda: remote(src.at[:, G - 1:G, J - 1, lower], lh.at[p, :, 0:1, lower], col_s.at[0], col_r.at[p, 0], where_to(0, fn))))
+        a_own = lambda d: remote(aps.at[p, d, :, 1:G], ap.at[p, :, 0:G - 1], line_s.at[0], a_r.at[p], where_to(d, f))
+        a_oth = lambda d: remote(aps.at[p, d, :, 0:1], ap.at[p, :, G - 1:G], line_s.at[1], a_r.at[p], where_to(d, fp))
+        b_own = lambda d: remote(aps.at[p, d, :, 0:G - 1], bm.at[p, :, 1:G], line_s.at[0], b_r.at[p], where_to(d, f))
+        b_oth = lambda d: remote(aps.at[p, d, :, G - 1:G], bm.at[p, :, 0:1], line_s.at[1], b_r.at[p], where_to(d, fn))
+        t_own = lambda d: remote(rows.at[p, 0, :, 0:G - 1], tr.at[p, d, :, 1:G], t_s.at[0], row_r.at[p, 0], where_to(0, f))
+        t_oth = lambda d: remote(rows.at[p, 0, :, G - 1:G], tr.at[p, d, :, 0:1], t_s.at[0], row_r.at[p, 1], where_to(0, fn))
+        d_own = lambda d: remote(rows.at[p, 1, :, 1:G], dr.at[p, d, :, 0:G - 1], d_s.at[0], row_r.at[p, 0], where_to(n_t - 1, f))
+        d_oth = lambda d: remote(rows.at[p, 1, :, 0:1], dr.at[p, d, :, G - 1:G], d_s.at[0], row_r.at[p, 1], where_to(n_t - 1, fp))
         return right, left, seam, a_own, a_oth, b_own, b_oth, t_own, t_oth, d_own, d_oth
 
     def stage(p, kind, src):
@@ -95,7 +96,7 @@
             for d in range(n_t):
                 aps[p, d, kind] = al[kind, :, 15 + d * J:15 + d * J + E, :]
 
-    def start(p, src):
+    def start_far(p, src):
         right, left, seam, a_own, a_oth, b_own, b_oth, t_own, t_oth, d_own, d_oth = copies(p, src)
 
         @pl.when(first)
@@ -137,6 +138,9 @@
             def _():
                 d_own(t).start()
 
+    def start_near(p, src):
+        right, left = copies(p, src)[0:2]
+
         @pl.when(inner_right)
         def _():
             right().start()
@@ -146,29 +150,34 @@
             left().start()
 
     def await_arrivals(p, src):
-        right, left, seam, a_own, a_oth, b_own, b_oth, t_own, t_oth, d_own, d_oth = copies(p, src)
+        right, left = copies(p, src)[0:2]
 
         @pl.when(inner_left)
         def _():
             right().wait_recv()
-            if G > 1:
-                a_own(0).wait_recv()
+            settle(ap.at[p], a_r.at[p])
+
+        @pl.when(first)
+        def _():
+            settle(ap.at[p, :, G - 1:G], a_r.at[p])
 
         @pl.when(inner_right)
         def _():
             left().wait_recv()
-            if G > 1:
-                b_own(0).wait_recv()
-
-        a_oth(0).wait_recv()
-        b_oth(0).wait_recv()
-
-    def await_seam(p, src):
-        seam = copies(p, src)[2]
-        for cond, make in seam:
-            @pl.when(last if cond is first else first)
-            def _(make=make):
-                make().wait_recv()
+            settle(bm.at[p], b_r.at[p])
+
+        @pl.when(last)
+        def _():
+            settle(bm.at[p, :, 0:1], b_r.at[p])
+
+    def await_seam(p):
+        @pl.when(last)
+        def _():
+            settle(rh.at[p, :, :, upper], col_r.at[p, 1])
+
+        @pl.when(first)
+        def _():
+            settle(lh.at[p, :, :, lower], col_r.at[p, 0])
 
         @pl.when(first)
         def _():
@@ -187,32 +196,33 @@
                 dl[:, :, 8 + d * J:8 + (d + 1) * J, :] = dr[p, d]
 
     def await_sends(p, src):
-        right, left, seam, a_own, a_oth, b_own, b_oth, t_own, t_oth, d_own, d_oth = copies(p, src)
+        right, left = copies(p, src)[0:2]
 
         @pl.when(inner_right)
         def _():
             right().wait_send()
+            settle(rows.at[p, 1], d_s.at[0])
+
+        @pl.when(last)
+        def _():
+            settle(src.at[:, :, J - 1, lower], col_s.at[0])
+            settle(rows.at[p, 1, :, 0:1], d_s.at[0])
+
+        @pl.when(inner_left)
+        def _():
+            left().wait_send()
+            settle(rows.at[p, 0], t_s.at[0])
+
+        @pl.when(first)
+        def _():
+            settle(src.at[:, :, 0, upper], col_s.at[1])
+            settle(rows.at[p, 0, :, G - 1:G], t_s.at[0])
+
+        @pl.when(jnp.logical_or(first, last))
+        def _():
             if G > 1:
-                d_own(t).wait_send()
-
-        @pl.when(inner_left)
-        def _():
-            left().wait_send()
-            if G > 1:
-                t_own(t).wait_send()
-
-        for cond, make in seam:
-            @pl.when(cond)
-            def _(make=make):
-                make().wait_send()
-        t_oth(t).wait_send()
-        d_oth(t).wait_send()
-
-        @pl.when(jnp.logical_or(first, last))
-        def _():
-            if G > 1:
-                settle(aps.at[p, 1:n_t, :, 1:G], line_s.at[p, 0])
-            settle(aps.at[p, :, :, 0:1], line_s.at[p, 1])
+                settle(aps.at[p, 1:n_t, :, 1:G], line_s.at[0])
+            settle(aps.at[p, :, :, 0:1], line_s.at[1])
 
     def fill_columns(src):
         for q in range(G):
@@ -254,7 +264,8 @@
                 for q in range(G):
                     for j in range(J):
                         m = (q * J + j) * H
-                        out[3 * a + b, m:m + H, :] = pad[q, j + a, 7 + b:7 + b + H, :].astype(BF16)
+                        n = 3 * a + b
+                        out[m:m + H, n * W:n * W + C] = pad[q, j + a, 7 + b:7 + b + H, :].astype(BF16)
 
     def forward_edge(p, q, j):
         if j == 0:
@@ -276,8 +287,9 @@
                     more = total[m:m + H, :]
                     for b in range(3):
                         tap = pad[q, j, 7 + b:7 + b + H, :].astype(BF16)
-                        more = more + product(tap, k[a, b], 1, 0)
-                        out[3 * a + b, m:m + H, :] += tap
+                        n = 3 * a + b
+                        more = more + product(tap, k[n * W:n * W + C], 1, 0)
+                        out[m:m + H, n * W:n * W + C] += tap
                     total[m:m + H, :] = more
 
     def backward_taps(p, src, out, late):
@@ -317,13 +329,16 @@
                     out[6 + b, m + H - 1:m + H, :] += low[j + 2 - b:j + 3 - b]
         if not late:
             backward_late(p, out, None, None)
+        for n in range(9):
+            xc[:, n * W:n * W + C] = out[n].astype(BF16)
 
     def backward_late(p, out, k, total):
         def add(n, m, rows_at, value):
-            out[n, m + rows_at.start:m + rows_at.stop, :] += value
+            here = slice(m + rows_at.start, m + rows_at.stop)
+            out[n, here, :] += value
             if total is not None:
-                here = slice(m + rows_at.start, m + rows_at.stop)
-                total[here, :] += product(value.astype(BF16), k[n // 3, n % 3], 1, 1)
+                xc[here, n * W:n * W + C] = out[n, here, :].astype(BF16)
+                total[here, :] += product(value.astype(BF16), k[n * W:n * W + C], 1, 0)
 
         @pl.when(last)
         def _():
@@ -345,14 +360,17 @@
                     add(3 * e, m, slice(0, S), tl[1, q, 9 - e:9 - e + S, :])
                     add(6 + e, m, slice(S, H), pad[q, 0, 9 - e:9 - e + 2 * S, :])
 
-    def apply(taps, k, dim):
-        total = product(taps[0].astype(BF16), k[0, 0], 1, dim)
-        for n in range(1, 9):
-            total = total + product(taps[n].astype(BF16), k[n // 3, n % 3], 1, dim)
-        return total
-
-    def flat(src):
-        return jnp.concatenate([src[q, j] for q in range(G) for j in range(J)], axis=0)
+    def lay_out(k, w):
+        for n in range(9):
+            tap = k[n // 3, n % 3]
+            kf[w, n * W:n * W + C] = tap
+            kb[w, n * W:n * W + C] = tap.astype(F32).T.astype(BF16)
+            if W > C:
+                kf[w, n * W + C:n * W + W] = jnp.zeros((W - C, C), BF16)
+                kb[w, n * W + C:n * W + W] = jnp.zeros((W - C, C), BF16)
+
+    def apply(taps, k):
+        return product(taps[...], k[...], 1, 0)
 
     def unflat(value, dst):
         for q in range(G):
@@ -424,7 +442,7 @@
                 mine = pl.ds(at + own * part, part)
                 sbuf[w, piece] = acc[w, piece].astype(BF16)
                 for digit, dev in found:
-                    remote(sbuf.at[w, piece], inbox.at[w, mine], w_s.at[w, self.sem], w_r.at[w, self.sem], dev).start()
+                    remote(sbuf.at[w, piece], inbox.at[w, mine], w_s.at[w], w_r.at[w, self.sem], dev).start()
                 inbox[w, mine] = sbuf[w, piece]
                 self.used[full] += part * (len(found) + 1)
                 return
@@ -437,7 +455,7 @@
                     out = sbuf.at[w, pl.ds(give, part)]
                 at = self.used[full]
                 self.used[full] += part
-                remote(out, inbox.at[w, at:at + part], w_s.at[w, self.sem], w_r.at[w, self.sem], dev).start()
+                remote(out, inbox.at[w, at:at + part], w_s.at[w], w_r.at[w, self.sem], dev).start()
             keep = self.lo + own * part
             self.done.append((keep, part, found))
             self.lo, self.length = keep, part
@@ -445,7 +463,7 @@
         def end(self):
             inbox, at, part, count, whole = self.flying
             sent = inbox.at[self.w, at:at + count * part]
-            settle(sent, w_s.at[self.w, self.sem])
+            settle(sent, w_s.at[self.w])
             settle(sent, w_r.at[self.w, self.sem])
             self.sem += 1
             terms = [inbox[self.w, at + n * part:at + (n + 1) * part].astype(F32) for n in range(count + whole)]
@@ -462,12 +480,12 @@
             self.flying = (part, len(found))
             for digit, dev in found:
                 remote(obuf.at[self.w, pl.ds(keep, part)], obuf.at[self.w, pl.ds(keep, part)],
-                       w_s.at[self.w, self.sem], w_r.at[self.w, self.sem], dev).start()
+                       w_s.at[self.w], w_r.at[self.w, self.sem], dev).start()
 
         def given(self):
             part, count = self.flying
             whole = obuf.at[self.w, 0:count * part]
-            settle(whole, w_s.at[self.w, self.sem])
+            settle(whole, w_s.at[self.w])
             settle(whole, w_r.at[self.w, self.sem])
             self.sem += 1
 
@@ -493,8 +511,9 @@
                 self.over = True
 
     barrier = pltpu.get_barrier_semaphore()
-    loads = [pltpu.make_async_copy(src, dst, in_s.at[n]) for n, (src, dst) in enumerate(
-        ((fields_h, raw.at[0]), (upstream_h, raw.at[1]), (k1_h, k1), (k2_h, k2)))]
+    loads = [pltpu.make_async_copy(src, dst, sem) for src, dst, sem in (
+        (fields_h, raw.at[0], w_s.at[0]), (upstream_h, raw.at[1], w_s.at[1]),
+        (k1_h, k1, line_s.at[0]), (k2_h, k2, line_s.at[1]))]
     for load in loads:
         load.start()
 
@@ -520,46 +539,53 @@
             acc[w, tiles * per:blocks] = jnp.zeros((blocks - tiles * per, 16, LANES), F32)
     pl.semaphore_wait(barrier, n_t * n_f - 1)
 
-    start(0, x)
     loads[2].wait()
     loads[3].wait()
+    start_far(0, x)
+    start_near(0, x)
+    lay_out(k1, 0)
+    lay_out(k2, 1)
+    for taps in (xf1, xf2, xc):
+        taps[...] = jnp.zeros_like(taps)
     await_arrivals(0, x)
     forward_taps(0, x.at[0], xf1, True)
-    pre[...] = apply(xf1, k1, 0)
+    pre[...] = apply(xf1, kf.at[0])
     backward_taps(0, x.at[1], xb, True)
-    back[...] = apply(xb, k2, 1)
-    await_seam(0, x)
-    forward_late(0, xf1, k1, pre)
-    backward_late(0, xb, k2, back)
+    back[...] = apply(xc, kb.at[1])
+    await_seam(0)
+    forward_late(0, xf1, kf.at[0], pre)
+    backward_late(0, xb, kb.at[1], back)
     value, slope = gelu_parts(pre[...])
-    unflat(value.astype(BF16), hidden)
+    cells = value.astype(BF16)
+    unflat(cells, hidden)
+    one, two = Sum(0, w1_o), Sum(1, w2_o)
+    wide = product(cells, xc[...], 0, 0)
+    pack([wide[:, n * W:n * W + C] * scale for n in range(9)], 1)
+    two.advance()
     cot = (back[...] * slope).astype(BF16)
     unflat(cot, pre_grad)
-    one, two = Sum(0, w1_o), Sum(1, w2_o)
-    cells = flat(hidden)
-    pack([product(cells, xb[n].astype(BF16), 0, 0) * scale for n in range(9)], 1)
-    two.advance()
-    pack([product(xf1[n], cot, 0, 0) * scale for n in range(9)], 0)
+    pack([product(xf1[:, n * W:n * W + C], cot, 0, 0) * scale for n in range(9)], 0)
     one.advance()
     two.advance()
     one.advance()
+    await_sends(0, x)
     stage(1, 0, y)
     stage(1, 1, y)
-    start(1, y)
+    start_far(1, y)
     two.advance()
     one.advance()
+    start_near(1, y)
     two.advance()
     one.advance()
     await_arrivals(1, y)
-    await_seam(1, y)
+    await_seam(1)
     forward_taps(1, hidden, xf2, False)
-    channel_major(apply(xf2, k2, 0), res_o)
+    channel_major(apply(xf2, kf.at[1]), res_o)
     backward_taps(1, pre_grad, xb, False)
-    channel_major(apply(xb, k1, 1), fg_o)
+    channel_major(apply(xc, kb.at[0]), fg_o)
     while not (one.over and two.over):
         two.advance()
         one.advance()
-    await_sends(0, x)
     await_sends(1, y)
 
 
@@ -593,6 +619,7 @@
     S = H // 3
     E = J + 2
     M = G * J * H
+    W = -(-C // LANES) * LANES
     scale = 1.0 / (S * 12.0 ** 0.5)
     groups = plan(n_t, n_f)
     cuts, stages = 1, 0
@@ -642,8 +669,11 @@
             pltpu.VMEM((2, G, S + 32, C), F32),
             pltpu.VMEM((G, J + 2, H + 16, C), F32),
             pltpu.VMEM((9, M, C), F32),
-            pltpu.VMEM((9, M, C), BF16),
-            pltpu.VMEM((9, M, C), BF16),
+            pltpu.VMEM((M, 9 * W), BF16),
+            pltpu.VMEM((M, 9 * W), BF16),
+            pltpu.VMEM((M, 9 * W), BF16),
+            pltpu.VMEM((2, 9 * W, C), BF16),
+            pltpu.VMEM((2, 9 * W, C), BF16),
             pltpu.VMEM((M, C), F32),
             pltpu.VMEM((M, C), F32),
             pltpu.VMEM((2, blocks, 16, LANES), F32),
@@ -651,10 +681,10 @@
             pltpu.VMEM((2, room[0], 16, LANES), BF16),
             pltpu.VMEM((2, room[1], 16, LANES), F32),
             pltpu.VMEM((2, blocks, 16, LANES), BF16),
-            dma((2, 4)), dma((2, 4)),
-            dma((2, 2)), dma((2, 2)), dma((2, 2)),
-            dma((2, 2)), dma((2, 2)), dma((2, 2)),
-            dma((2, stages)), dma((2, stages)), dma((4,)),
+            dma((2,)), dma((2, 2)),
+            dma((2,)), dma((2,)), dma((2,)),
+            dma((1,)), dma((1,)), dma((2, 2)),
+            dma((2,)), dma((2, stages)),
         ],
         compiler_params=pltpu.CompilerParams(
             collective_id=0, has_side_effects=True, vmem_limit_bytes=24 * 1024 * 1024),

time: 30.4 us -> 29.3 us (0.964)
  Pallas kernels: 29.6 us -> 28.5 us
    pallas_call x1, Pallas kernels: 28.6 us -> 27.5 us  [run(): pl.pallas_call(functools.partial(body, n_t, n_f, scale, groups), out_shap...]
where the time goes in v4:
time: 29.3 us; the launch traced here: 29.2 us
  Pallas kernels  28.5 us (97%)
  between operations  0.64 us (2%)
    pallas_call x1, Pallas kernels, run(): pl.pallas_call(functools.partial(body, n_t, n_f, scale, groups), out_shap...  27.5 us
    pallas_call x1, Pallas kernels, send_out(): pl.pallas_call(deliver, out_shape=[jax.ShapeDtypeStruct(a.shape, a.dtype)...  1.01 us

profile of v4, /device:TPU:0, one launch (start us, length us, event | category | flops | bytes accessed | tf_op | source)
XLA Modules:
  0.0 29.2 jit_solution(9702692525183227114)
XLA Ops:
  0.6 27.5 %shard_map.75 = (bf16[96,2,2,96]{3,2,1,0:T(2,128)(2,1)S(1)}, bf16[96,2,2,96]{3,2,1,0:T(2,128)(2,1)S(1)}, f32[3,3,96,96]{3,2,1,0:T(8,128)S(1)}, f32[3,3,96,96]{3,2,1,0:T(8,128)S(1)}) custom-call(bf16[96,2,2,96]{3,2,1,0:T(2,128)(2,1)} %fields_h.1, bf16[96,2,2,96]{3,2,1,0:T(2,128)(2,1)} %upstream_h.1, bf16[3,3,96,96]{3,2,1,0:T(8,128)(2,1)} %k1_h.1, ...), custom_call_target="tpu_custom_call" | custom-call | tf_op jit(solution)/shard_map/pallas_call | solution.py:643
  28.2 1.0 %shard_map.76 = (bf16[96,2,2,96]{3,2,1,0:T(2,128)(2,1)}, bf16[96,2,2,96]{3,2,1,0:T(2,128)(2,1)}, f32[3,3,96,96]{3,2,1,0:T(8,128)}, f32[3,3,96,96]{3,2,1,0:T(8,128)}) custom-call(bf16[96,2,2,96]{3,2,1,0:T(2,128)(2,1)S(1)} %get-tuple-element.8.refs_0_, bf16[96,2,2,96]{3,2,1,0:T(2,128)(2,1)S(1)} %get-tuple-element.9.refs_1_, ...), custom_call_target="tpu_custom_call" | custom-call | tf_op jit(solution)/shard_map/pallas_call | solution.py:697

commit v5 on v4

--- a/solution.py
+++ b/solution.py
@@ -27,7 +27,7 @@
 
 
 def body(n_t, n_f, scale, groups, fields_h, upstream_h, k1_h, k2_h, res_o, fg_o, w1_o, w2_o,
-         raw, x, k1, k2, y, rows, lh, rh, ap, bm, aps, tr, dr, tl, dl, al, pad, xb, xf1, xf2, xc, kf, kb, pre, back,
+         raw, x, k1, k2, y, rows, lh, rh, ap, bm, aps, tr, dr, tl, dl, al, pad, xb, xf1, xf2, xc, kf, kb, kl, lm, pad2, pre, back,
          acc, sbuf, rlow, rfull, obuf,
          col_s, col_r, line_s, a_r, b_r, t_s, d_s, row_r, w_s, w_r):
     _, G, J, H, C = x.shape
@@ -360,6 +360,114 @@
                     add(3 * e, m, slice(0, S), tl[1, q, 9 - e:9 - e + S, :])
                     add(6 + e, m, slice(S, H), pad[q, 0, 9 - e:9 - e + 2 * S, :])
 
+    def own_forward(src, k, out, total):
+        fill_columns(src)
+        for q in range(G):
+            for j in (0, J + 1):
+                pad[q, j, :, :] = jnp.zeros((H + 16, C), F32)
+            for j in range(1, J + 1):
+                pad[q, j, 7:8, :] = jnp.zeros((1, C), F32)
+                pad[q, j, 8 + H:9 + H, :] = jnp.zeros((1, C), F32)
+        for a in range(3):
+            for b in range(3):
+                for q in range(G):
+                    for j in range(J):
+                        m, n = (q * J + j) * H, 3 * a + b
+                        out[m:m + H, n * W:n * W + C] = pad[q, j + a, 7 + b:7 + b + H, :].astype(BF16)
+        total[...] = apply(out, k)
+
+    def more_forward(p, k, out, total):
+        for q in range(G):
+            @pl.when(inner_left)
+            def _():
+                pad[q, 0, 8:8 + H, :] = lh[p, 0, q].astype(F32)
+
+            @pl.when(inner_right)
+            def _():
+                pad[q, J + 1, 8:8 + H, :] = rh[p, 0, q].astype(F32)
+            for j in range(E):
+                pad[q, j, 7:8, :] = ap[p, 0, q, j:j + 1]
+                pad[q, j, 8 + H:9 + H, :] = bm[p, 0, q, j:j + 1]
+        for q in range(G):
+            for j in range(J):
+                r = q * J + j
+                m = r * H
+                for a in range(3):
+                    e = j + a
+                    if e == 0 or e == J + 1:
+                        for b in range(3):
+                            n = 3 * a + b
+                            out[m:m + H, n * W:n * W + C] = pad[q, e, 7 + b:7 + b + H, :].astype(BF16)
+                        wide = slice(3 * a * W, 3 * (a + 1) * W)
+                        total[m:m + H, :] += product(out[m:m + H, wide], k[wide], 1, 0)
+                    else:
+                        n = 3 * a
+                        out[m:m + 16, n * W:n * W + C] = pad[q, e, 7:23, :].astype(BF16)
+                        n = 3 * a + 2
+                        out[m + H - 16:m + H, n * W:n * W + C] = pad[q, e, H - 7:H + 9, :].astype(BF16)
+                        lm[0, r:r + 1, a * W:a * W + C] = ap[p, 0, q, e:e + 1]
+                        lm[1, r:r + 1, a * W:a * W + C] = bm[p, 0, q, e:e + 1]
+        add_lines(0, kl[0], kl[1], total)
+
+    def add_lines(at, k_top, k_low, total):
+        top = product(lm[at].astype(BF16), k_top, 1, 0)
+        low = product(lm[at + 1].astype(BF16), k_low, 1, 0)
+        for r in range(G * J):
+            m = r * H
+            total[m:m + 1, :] += top[r:r + 1]
+            total[m + H - 1:m + H, :] += low[r:r + 1]
+
+    def own_backward(src, k, out, total):
+        for q in range(G):
+            for j in (0, J + 1):
+                pad2[q, j, :, :] = jnp.zeros((H + 16, C), F32)
+            for j in range(J):
+                pad2[q, 1 + j, 8:8 + H, :] = src[q, j].astype(F32)
+                pad2[q, 1 + j, 7:8, :] = jnp.zeros((1, C), F32)
+                pad2[q, 1 + j, 8 + H:9 + H, :] = jnp.zeros((1, C), F32)
+        for a in range(3):
+            for b in range(3):
+                n = 3 * a + b
+                for q in range(G):
+                    for j in range(J):
+                        m = (q * J + j) * H
+                        out[n, m:m + H, :] = pad2[q, j - a + 2, 9 - b:9 - b + H, :]
+                xc[:, n * W:n * W + C] = out[n].astype(BF16)
+        total[...] = apply(xc, k)
+
+    def more_backward(p, k, out, total):
+        for q in range(G):
+            @pl.when(inner_left)
+            def _():
+                pad2[q, 0, 8:8 + H, :] = lh[p, 1, q].astype(F32)
+
+            @pl.when(inner_right)
+            def _():
+                pad2[q, J + 1, 8:8 + H, :] = rh[p, 1, q].astype(F32)
+        for q in range(G):
+            top = ap[p, 1, q]
+            low = bm[p, 1, q]
+            for j in range(J):
+                r = q * J + j
+                m = r * H
+                for a, line, at, lines in ((0, 0, 2, top), (2, H - 1, 3, low)):
+                    e = j - a + 2
+                    outer = e == 0 or e == J + 1
+                    for b in range(3):
+                        n = 3 * a + b
+                        add = lines[j + 2 - b:j + 3 - b]
+                        if outer:
+                            out[n, m:m + H, :] = pad2[q, e, 9 - b:9 - b + H, :]
+                        else:
+                            lm[at, r:r + 1, b * W:b * W + C] = add
+                        out[n, m + line:m + line + 1, :] += add
+                        span = slice(m, m + H) if outer else slice(m, m + 16) if a == 0 else slice(m + H - 16, m + H)
+                        xc[span, n * W:n * W + C] = out[n, span, :].astype(BF16)
+                    if outer:
+                        wide = slice(3 * a * W, 3 * (a + 1) * W)
+                        total[m:m + H, :] += product(xc[m:m + H, wide], k[wide], 1, 0)
+        add_lines(2, k[0:3 * W], k[6 * W:9 * W], total)
+
     def lay_out(k, w):
         for n in range(9):
             tap = k[n // 3, n % 3]
@@ -380,9 +488,8 @@
 
     def channel_major(value, dst):
         for q in range(G):
-            for j in range(J):
-                m = (q * J + j) * H
-                dst[:, q, j, :] = value[m:m + H].T.astype(BF16)
+            sides = [value[(q * J + j) * H:(q * J + j + 1) * H].T.astype(BF16) for j in range(J)]
+            dst[:, q, :, :] = jnp.stack(sides, axis=1)
 
     per = C // 16
     tiles = -(-9 * C // LANES)
@@ -545,13 +652,18 @@
     start_near(0, x)
     lay_out(k1, 0)
     lay_out(k2, 1)
+    for a in range(3):
+        for side in range(2):
+            n = 3 * a + 2 * side
+            kl[side, a * W:(a + 1) * W] = kf[0, n * W:(n + 1) * W]
+    lm[...] = jnp.zeros_like(lm)
     for taps in (xf1, xf2, xc):
         taps[...] = jnp.zeros_like(taps)
+    own_forward(x.at[0], kf.at[0], xf1, pre)
+    own_backward(x.at[1], kb.at[1], xb, back)
     await_arrivals(0, x)
-    forward_taps(0, x.at[0], xf1, True)
-    pre[...] = apply(xf1, kf.at[0])
-    backward_taps(0, x.at[1], xb, True)
-    back[...] = apply(xc, kb.at[1])
+    more_forward(0, kf.at[0], xf1, pre)
+    more_backward(0, kb.at[1], xb, back)
     await_seam(0)
     forward_late(0, xf1, kf.at[0], pre)
     backward_late(0, xb, kb.at[1], back)
@@ -674,6 +786,9 @@
             pltpu.VMEM((M, 9 * W), BF16),
             pltpu.VMEM((2, 9 * W, C), BF16),
             pltpu.VMEM((2, 9 * W, C), BF16),
+            pltpu.VMEM((2, 3 * W, C), BF16),
+            pltpu.VMEM((4, -(-G * J // 16) * 16, 3 * W), F32),
+            pltpu.VMEM((G, J + 2, H + 16, C), F32),
             pltpu.VMEM((M, C), F32),
             pltpu.VMEM((M, C), F32),
             pltpu.VMEM((2, blocks, 16, LANES), F32),

time: 29.3 us -> 29.4 us (level)
  no operation moved by 1% of the time
where the time goes in v5:
time: 29.4 us; the launch traced here: 29.2 us
  Pallas kernels  28.6 us (97%)
  between operations  0.64 us (2%)
    pallas_call x1, Pallas kernels, run(): pl.pallas_call(functools.partial(body, n_t, n_f, scale, groups), out_shap...  27.6 us
    pallas_call x1, Pallas kernels, send_out(): pl.pallas_call(deliver, out_shape=[jax.ShapeDtypeStruct(a.shape, a.dtype)...  1.01 us

profile of v5, /device:TPU:0, one launch (start us, length us, event | category | flops | bytes accessed | tf_op | source)
XLA Modules:
  0.0 29.2 jit_solution(11589390972310000087)
XLA Ops:
  0.6 27.6 %shard_map.75 = (bf16[96,2,2,96]{3,2,1,0:T(2,128)(2,1)S(1)}, bf16[96,2,2,96]{3,2,1,0:T(2,128)(2,1)S(1)}, f32[3,3,96,96]{3,2,1,0:T(8,128)S(1)}, f32[3,3,96,96]{3,2,1,0:T(8,128)S(1)}) custom-call(bf16[96,2,2,96]{3,2,1,0:T(2,128)(2,1)} %fields_h.1, bf16[96,2,2,96]{3,2,1,0:T(2,128)(2,1)} %upstream_h.1, bf16[3,3,96,96]{3,2,1,0:T(8,128)(2,1)} %k1_h.1, ...), custom_call_target="tpu_custom_call" | custom-call | tf_op jit(solution)/shard_map/pallas_call | solution.py:755
  28.2 1.0 %shard_map.76 = (bf16[96,2,2,96]{3,2,1,0:T(2,128)(2,1)}, bf16[96,2,2,96]{3,2,1,0:T(2,128)(2,1)}, f32[3,3,96,96]{3,2,1,0:T(8,128)}, f32[3,3,96,96]{3,2,1,0:T(8,128)}) custom-call(bf16[96,2,2,96]{3,2,1,0:T(2,128)(2,1)S(1)} %get-tuple-element.8.refs_0_, bf16[96,2,2,96]{3,2,1,0:T(2,128)(2,1)S(1)} %get-tuple-element.9.refs_1_, ...), custom_call_target="tpu_custom_call" | custom-call | tf_op jit(solution)/shard_map/pallas_call | solution.py:812

commit v6 on v5

--- a/solution.py
+++ b/solution.py
@@ -43,7 +43,7 @@
     inner_left = jnp.logical_not(first)
     inner_right = jnp.logical_not(last)
 
-    upper, lower = slice(S - 16, H), slice(0, 2 * S + 16)
+    upper, lower = slice(S, H), slice(0, 2 * S)
 
     def where_to(tile, face):
         return {"tile": tile, "face": face}
@@ -98,35 +98,53 @@
 
     def start_far(p, src):
         right, left, seam, a_own, a_oth, b_own, b_oth, t_own, t_oth, d_own, d_oth = copies(p, src)
+        half = n_t // 2
 
         @pl.when(first)
         def _():
-            @pl.loop(0, n_t)
+            @pl.loop(0, n_t - half)
             def _(d):
                 a_oth(n_t - 1 - d).start()
-            if G > 1:
-                @pl.loop(1, n_t)
-                def _(d):
-                    a_own(n_t - d).start()
-                ap[p, :, 0:G - 1] = aps[p, 0, :, 1:G]
-                tr[p, 0, :, 1:G] = rows[p, 0, :, 0:G - 1]
+                if G > 1:
+                    a_own(n_t - 1 - d).start()
 
         @pl.when(last)
         def _():
-            @pl.loop(0, n_t)
+            @pl.loop(0, half)
             def _(d):
                 b_oth(d).start()
-            if G > 1:
-                @pl.loop(0, n_t - 1)
-                def _(d):
+                if G > 1:
                     b_own(d).start()
-                bm[p, :, 1:G] = aps[p, n_t - 1, :, 0:G - 1]
-                dr[p, n_t - 1, :, 0:G - 1] = rows[p, 1, :, 1:G]
-
         for cond, make in seam:
             @pl.when(cond)
             def _(make=make):
                 make().start()
+
+        @pl.when(first)
+        def _():
+            a_oth(0).start()
+
+            @pl.loop(1, half)
+            def _(d):
+                a_oth(half - d).start()
+                if G > 1:
+                    a_own(half - d).start()
+            if G > 1:
+                ap[p, :, 0:G - 1] = aps[p, 0, :, 1:G]
+                tr[p, 0, :, 1:G] = rows[p, 0, :, 0:G - 1]
+
+        @pl.when(last)
+        def _():
+            b_oth(n_t - 1).start()
+
+            @pl.loop(half, n_t - 1)
+            def _(d):
+                b_oth(d).start()
+                if G > 1:
+                    b_own(d).start()
+            if G > 1:
+                bm[p, :, 1:G] = aps[p, n_t - 1, :, 0:G - 1]
+                dr[p, n_t - 1, :, 0:G - 1] = rows[p, 1, :, 1:G]
         t_oth(t).start()
         d_oth(t).start()
         if G > 1:
@@ -281,16 +299,12 @@
             def _(a=a, j=j):
                 for q in range(G):
                     forward_edge(p, q, j)
-                    pad[q, j, 7:8, :] = jnp.zeros((1, C), F32)
-                    pad[q, j, 8 + H:9 + H, :] = jnp.zeros((1, C), F32)
                     m = (q * J + j - a) * H
-                    more = total[m:m + H, :]
                     for b in range(3):
-                        tap = pad[q, j, 7 + b:7 + b + H, :].astype(BF16)
                         n = 3 * a + b
-                        more = more + product(tap, k[n * W:n * W + C], 1, 0)
-                        out[m:m + H, n * W:n * W + C] += tap
-                    total[m:m + H, :] = more
+                        out[m:m + H, n * W:n * W + C] = pad[q, j, 7 + b:7 + b + H, :].astype(BF16)
+                    wide = slice(3 * a * W, 3 * (a + 1) * W)
+                    total[m:m + H, :] += product(out[m:m + H, wide], k[wide], 1, 0)
 
     def backward_taps(p, src, out, late):
         fill_columns(src)
@@ -344,7 +358,8 @@
         def _():
             for q in range(G):
                 m = (q * J + J - 1) * H
-                pad[q, J + 1, 8:8 + H, :] = rh[p, 1, q].astype(F32)
+                pad[q, J + 1, 8 + S:8 + H, :] = rh[p, 1, q, S:H].astype(F32)
+                pad[q, J + 1, 7 + S:8 + S, :] = ap[p, 1, q, J:J + 1]
                 pad[q, J + 1, 8 + H:9 + H, :] = jnp.zeros((1, C), F32)
                 for e in range(3):
                     add(e, m, slice(0, 2 * S), pad[q, J + 1, 8 + S + 1 - e:8 + H + 1 - e, :])
@@ -355,7 +370,8 @@
             for q in range(G):
                 m = q * J * H
                 pad[q, 0, 7:8, :] = jnp.zeros((1, C), F32)
-                pad[q, 0, 8:8 + H, :] = lh[p, 1, q].astype(F32)
+                pad[q, 0, 8:8 + 2 * S, :] = lh[p, 1, q, 0:2 * S].astype(F32)
+                pad[q, 0, 8 + 2 * S:9 + 2 * S, :] = bm[p, 1, q, 1:2]
                 for e in range(3):
                     add(3 * e, m, slice(0, S), tl[1, q, 9 - e:9 - e + S, :])
                     add(6 + e, m, slice(S, H), pad[q, 0, 9 - e:9 - e + 2 * S, :])

time: 29.4 us -> 29 us (0.986)
  Pallas kernels: 28.6 us -> 28.2 us
    pallas_call x1, Pallas kernels: 27.6 us -> 27.2 us  [run(): pl.pallas_call(functools.partial(body, n_t, n_f, scale, groups), out_shap...]
where the time goes in v6:
time: 29 us; the launch traced here: 28.8 us
  Pallas kernels  28.2 us (97%)
  between operations  0.64 us (2%)
    pallas_call x1, Pallas kernels, run(): pl.pallas_call(functools.partial(body, n_t, n_f, scale, groups), out_shap...  27.2 us
    pallas_call x1, Pallas kernels, send_out(): pl.pallas_call(deliver, out_shape=[jax.ShapeDtypeStruct(a.shape, a.dtype)...  1.01 us

profile of v6, /device:TPU:0, one launch (start us, length us, event | category | flops | bytes accessed | tf_op | source)
XLA Modules:
  0.0 28.8 jit_solution(9128617873150594443)
XLA Ops:
  0.6 27.2 %shard_map.75 = (bf16[96,2,2,96]{3,2,1,0:T(2,128)(2,1)S(1)}, bf16[96,2,2,96]{3,2,1,0:T(2,128)(2,1)S(1)}, f32[3,3,96,96]{3,2,1,0:T(8,128)S(1)}, f32[3,3,96,96]{3,2,1,0:T(8,128)S(1)}) custom-call(bf16[96,2,2,96]{3,2,1,0:T(2,128)(2,1)} %fields_h.1, bf16[96,2,2,96]{3,2,1,0:T(2,128)(2,1)} %upstream_h.1, bf16[3,3,96,96]{3,2,1,0:T(8,128)(2,1)} %k1_h.1, ...), custom_call_target="tpu_custom_call" | custom-call | tf_op jit(solution)/shard_map/pallas_call | solution.py:771
  27.8 1.0 %shard_map.76 = (bf16[96,2,2,96]{3,2,1,0:T(2,128)(2,1)}, bf16[96,2,2,96]{3,2,1,0:T(2,128)(2,1)}, f32[3,3,96,96]{3,2,1,0:T(8,128)}, f32[3,3,96,96]{3,2,1,0:T(8,128)}) custom-call(bf16[96,2,2,96]{3,2,1,0:T(2,128)(2,1)S(1)} %get-tuple-element.8.refs_0_, bf16[96,2,2,96]{3,2,1,0:T(2,128)(2,1)S(1)} %get-tuple-element.9.refs_1_, ...), custom_call_target="tpu_custom_call" | custom-call | tf_op jit(solution)/shard_map/pallas_call | solution.py:828

commit v7 on v6

--- a/solution.py
+++ b/solution.py
@@ -729,7 +729,7 @@
 def plan(n_t, n_f):
     tile_bits = [("tile", 1 << i) for i in range(n_t.bit_length() - 1)]
     face_bits = [("face", 1 << i) for i in range(n_f.bit_length() - 1)]
-    groups = [(tile_bits[:1], 1, 0)]
+    groups = [(tile_bits[:1], 0, 0)]
     middle, rest = face_bits + tile_bits[1:3], tile_bits[3:]
     while middle:
         groups.append((middle[:3], 0, 0))

time: 29 us -> 28.9 us (level)
  no operation moved by 1% of the time
where the time goes in v7:
time: 28.9 us; the launch traced here: 28.7 us
  Pallas kernels  28.1 us (97%)
  between operations  0.64 us (2%)
    pallas_call x1, Pallas kernels, run(): pl.pallas_call(functools.partial(body, n_t, n_f, scale, groups), out_shap...  27.1 us
    pallas_call x1, Pallas kernels, send_out(): pl.pallas_call(deliver, out_shape=[jax.ShapeDtypeStruct(a.shape, a.dtype)...  1.01 us

profile of v7, /device:TPU:0, one launch (start us, length us, event | category | flops | bytes accessed | tf_op | source)
XLA Modules:
  0.0 28.7 jit_solution(9691033255178559917)
XLA Ops:
  0.6 27.1 %shard_map.75 = (bf16[96,2,2,96]{3,2,1,0:T(2,128)(2,1)S(1)}, bf16[96,2,2,96]{3,2,1,0:T(2,128)(2,1)S(1)}, f32[3,3,96,96]{3,2,1,0:T(8,128)S(1)}, f32[3,3,96,96]{3,2,1,0:T(8,128)S(1)}) custom-call(bf16[96,2,2,96]{3,2,1,0:T(2,128)(2,1)} %fields_h.1, bf16[96,2,2,96]{3,2,1,0:T(2,128)(2,1)} %upstream_h.1, bf16[3,3,96,96]{3,2,1,0:T(8,128)(2,1)} %k1_h.1, ...), custom_call_target="tpu_custom_call" | custom-call | tf_op jit(solution)/shard_map/pallas_call | solution.py:771
  27.7 1.0 %shard_map.76 = (bf16[96,2,2,96]{3,2,1,0:T(2,128)(2,1)}, bf16[96,2,2,96]{3,2,1,0:T(2,128)(2,1)}, f32[3,3,96,96]{3,2,1,0:T(8,128)}, f32[3,3,96,96]{3,2,1,0:T(8,128)}) custom-call(bf16[96,2,2,96]{3,2,1,0:T(2,128)(2,1)S(1)} %get-tuple-element.8.refs_0_, bf16[96,2,2,96]{3,2,1,0:T(2,128)(2,1)S(1)} %get-tuple-element.9.refs_1_, ...), custom_call_target="tpu_custom_call" | custom-call | tf_op jit(solution)/shard_map/pallas_call | solution.py:828

commit v8 on v7

--- a/solution.py
+++ b/solution.py
@@ -699,8 +699,8 @@
     await_sends(0, x)
     stage(1, 0, y)
     stage(1, 1, y)
+    two.advance()
     start_far(1, y)
-    two.advance()
     one.advance()
     start_near(1, y)
     two.advance()

time: 28.9 us -> 28.9 us (level)
  no operation moved by 1% of the time
where the time goes in v8:
time: 28.9 us; the launch traced here: 28.7 us
  Pallas kernels  28.1 us (97%)
  between operations  0.64 us (2%)
    pallas_call x1, Pallas kernels, run(): pl.pallas_call(functools.partial(body, n_t, n_f, scale, groups), out_shap...  27.1 us
    pallas_call x1, Pallas kernels, send_out(): pl.pallas_call(deliver, out_shape=[jax.ShapeDtypeStruct(a.shape, a.dtype)...  1.01 us

profile of v8, /device:TPU:0, one launch (start us, length us, event | category | flops | bytes accessed | tf_op | source)
XLA Modules:
  0.0 28.7 jit_solution(16775481458356685034)
XLA Ops:
  0.6 27.1 %shard_map.75 = (bf16[96,2,2,96]{3,2,1,0:T(2,128)(2,1)S(1)}, bf16[96,2,2,96]{3,2,1,0:T(2,128)(2,1)S(1)}, f32[3,3,96,96]{3,2,1,0:T(8,128)S(1)}, f32[3,3,96,96]{3,2,1,0:T(8,128)S(1)}) custom-call(bf16[96,2,2,96]{3,2,1,0:T(2,128)(2,1)} %fields_h.1, bf16[96,2,2,96]{3,2,1,0:T(2,128)(2,1)} %upstream_h.1, bf16[3,3,96,96]{3,2,1,0:T(8,128)(2,1)} %k1_h.1, ...), custom_call_target="tpu_custom_call" | custom-call | tf_op jit(solution)/shard_map/pallas_call | solution.py:771
  27.7 1.0 %shard_map.76 = (bf16[96,2,2,96]{3,2,1,0:T(2,128)(2,1)}, bf16[96,2,2,96]{3,2,1,0:T(2,128)(2,1)}, f32[3,3,96,96]{3,2,1,0:T(8,128)}, f32[3,3,96,96]{3,2,1,0:T(8,128)}) custom-call(bf16[96,2,2,96]{3,2,1,0:T(2,128)(2,1)S(1)} %get-tuple-element.8.refs_0_, bf16[96,2,2,96]{3,2,1,0:T(2,128)(2,1)S(1)} %get-tuple-element.9.refs_1_, ...), custom_call_target="tpu_custom_call" | custom-call | tf_op jit(solution)/shard_map/pallas_call | solution.py:828
